TPU v7x, 32 devices: a whole 2x2x4 slice. The times are simulated.
32 devices in a mesh: dp: 4 (over y, x), fsdp: 8 (over z, core).
Axes of the slice: x: 2, y: 2, z: 4, core: 2. Of those that a mesh axis runs over, the one named last changes fastest.
Arguments:
- inputs: float32 [64, 256, 512], P(('dp', 'fsdp')), may hold values from -6 to 6
- cotangent: float32 [64, 256, 512], P(('dp', 'fsdp')), may hold values from -6 to 6
- segments: int32 [64, 256], P(('dp', 'fsdp')), may hold values from 0 to 7, never falling along the last dimension, each value on 1 to 96 neighbouring positions
- valid_mask: int32 [64, 256], P(('dp', 'fsdp')), may hold values 0 or 1
- step_count: int32 [1], replicated, may hold values from 1 to 20
- feed_in: float32 [2, 512, 2048], P(None, ('dp', 'fsdp')), may hold values from -0.25 to 0.25
- feed_out: float32 [2, 2048, 512], P(None, ('dp', 'fsdp')), may hold values from -0.125 to 0.125
- square_proj: float32 [6, 512, 512], P(None, ('dp', 'fsdp')), may hold values from -0.53033009 to 0.53033009
- conv_proj: float32 [512, 1024], P(('dp', 'fsdp')), may hold values from -0.25 to 0.25
- small_params: float32 [40, 512], P(None, ('dp', 'fsdp')), may hold values from -0.6 to 1.4
- feed_in_first: float32 [2, 512, 2048], P(None, ('dp', 'fsdp')), may hold values from -0.00061035156 to 0.00061035156
- feed_in_second: float32 [2, 512, 2048], P(None, ('dp', 'fsdp')), may hold values from 7.9214996e-11 to 1.2674399e-09
- feed_out_first: float32 [2, 2048, 512], P(None, ('dp', 'fsdp')), may hold values from -0.00061035156 to 0.00061035156
- feed_out_second: float32 [2, 2048, 512], P(None, ('dp', 'fsdp')), may hold values from 7.9214996e-11 to 1.2674399e-09
- square_first: float32 [6, 512, 512], P(None, ('dp', 'fsdp')), may hold values from -0.00061035156 to 0.00061035156
- square_second: float32 [6, 512, 512], P(None, ('dp', 'fsdp')), may hold values from 7.9214996e-11 to 1.2674399e-09
- conv_first: float32 [512, 1024], P(('dp', 'fsdp')), may hold values from -0.00061035156 to 0.00061035156
- conv_second: float32 [512, 1024], P(('dp', 'fsdp')), may hold values from 7.9214996e-11 to 1.2674399e-09
- small_first: float32 [40, 512], P(None, ('dp', 'fsdp')), may hold values from -0.00061035156 to 0.00061035156
- small_second: float32 [40, 512], P(None, ('dp', 'fsdp')), may hold values from 7.9214996e-11 to 1.2674399e-09
Outputs:
- layer_output: float32 [64, 256, 512], P(('dp', 'fsdp'))
- input_gradient: float32 [64, 256, 512], P(('dp', 'fsdp'))
- gradient_norm: float32 [], replicated
- feed_in_first_next: float32 [2, 512, 2048], P(None, ('dp', 'fsdp'))
- feed_in_second_next: float32 [2, 512, 2048], P(None, ('dp', 'fsdp'))
- feed_in_next: float32 [2, 512, 2048], P(None, ('dp', 'fsdp'))
- feed_out_first_next: float32 [2, 2048, 512], P(None, ('dp', 'fsdp'))
- feed_out_second_next: float32 [2, 2048, 512], P(None, ('dp', 'fsdp'))
- feed_out_next: float32 [2, 2048, 512], P(None, ('dp', 'fsdp'))
- square_first_next: float32 [6, 512, 512], P(None, ('dp', 'fsdp'))
- square_second_next: float32 [6, 512, 512], P(None, ('dp', 'fsdp'))
- square_next: float32 [6, 512, 512], P(None, ('dp', 'fsdp'))
- conv_first_next: float32 [512, 1024], P(('dp', 'fsdp'))
- conv_second_next: float32 [512, 1024], P(('dp', 'fsdp'))
- conv_next: float32 [512, 1024], P(('dp', 'fsdp'))
- small_first_next: float32 [40, 512], P(None, ('dp', 'fsdp'))
- small_second_next: float32 [40, 512], P(None, ('dp', 'fsdp'))
- small_next: float32 [40, 512], P(None, ('dp', 'fsdp'))
Inputs may be any that keep to these rules, and one draw needn't show every extreme that they name: `segments`: in each pack the utterance numbers never fall along the frames; each utterance has 1 to 96 frames, and one has exactly 96.
All inputs are finite; a program needn't handle non-finite values. No bound on the sum of `valid_mask` on one device may be relied on, other than what follows from the above.
Results may differ from a plain program's by a relative error of at most 0.0003.
Values sent between devices are 32-bit elements; how exact they have to be, the bound alone decides.
A program may use at most 256 MiB of HBM per device.

v0:
```python
import math

import jax
import jax.numpy as jnp
from jax import lax
from jax.sharding import PartitionSpec as P

D = 512
H = 8
DH = 64
FF = 2048
K = 9


PRECISE = lax.Precision.HIGHEST
NORM_EPS = 1e-05
BETA_ONE = 0.9
BETA_TWO = 0.999
ADAM_EPS = 1e-08
CLIP_NORM = 1.0
MATRIX_RATE = 0.03
VECTOR_RATE = 0.4
MATRIX_DECAY = 0.01


def matmul(left, right):
    return jnp.dot(left, right, precision=PRECISE, preferred_element_type=jnp.float32)


def swish_unit(values):
    return values * jax.nn.sigmoid(values)


def layer_norm(values, gain_row, bias_row):
    centred = values - jnp.mean(values, axis=-1, keepdims=True)
    variance = jnp.mean(centred * centred, axis=-1, keepdims=True)
    return centred * lax.rsqrt(variance + NORM_EPS) * gain_row + bias_row


def feed_forward(normed, weight_in, weight_out, bias_in, bias_out):
    return matmul(swish_unit(matmul(normed, weight_in) + bias_in), weight_out) + bias_out


def sinusoid(offsets):
    half_width = D // 2
    frequency = jnp.exp(
        jnp.arange(half_width, dtype=jnp.int32).astype(jnp.float32) * (-2.0 * math.log(10000.0) / D)
    )
    angles = offsets[:, None] * frequency[None, :]
    return jnp.concatenate([jnp.sin(angles), jnp.cos(angles)], axis=1)


def block_scores(arrays, block_item, length, block_rows):
    key_heads, value_heads, position_heads, segment, valid = arrays
    content_query, position_query, first_row = block_item
    content = jnp.einsum("ihc,jhc->hij", content_query, key_heads, precision=PRECISE)
    position_raw = jnp.einsum("ihc,shc->his", position_query, position_heads, precision=PRECISE)
    flattened = position_raw.reshape(H, block_rows * 2 * length)
    flattened = jnp.concatenate([flattened, jnp.zeros((H, length), jnp.float32)], axis=1)
    shifted = lax.dynamic_slice_in_dim(
        flattened, length - 1 - first_row, block_rows * (2 * length - 1), 1
    )
    relative = shifted.reshape(H, block_rows, 2 * length - 1)[:, :, :length]
    query_rows = first_row + jnp.arange(block_rows, dtype=jnp.int32)
    key_rows = jnp.arange(length, dtype=jnp.int32)
    same_segment = (segment[:, None] == segment[None, :]) & (valid[None, :] > 0)
    allowed = same_segment | (query_rows[:, None] == key_rows[None, :])
    scores = (content + relative) * (1.0 / math.sqrt(DH))
    scores = jnp.where(allowed[None, :, :], scores, -1e30)
    row_peak = jnp.max(scores, axis=-1, keepdims=True)
    weights = jnp.exp(scores - row_peak)
    weights = weights / jnp.sum(weights, axis=-1, keepdims=True)
    context = jnp.einsum("hij,jhc->ihc", weights, value_heads, precision=PRECISE)
    return context.reshape(block_rows, D)


def attention(normed, segment, valid, square, small_rows):
    length = normed.shape[0]
    block_rows = min(512, length)
    block_count = length // block_rows
    queries = matmul(normed, square[0]) + small_rows[12]
    key_heads = matmul(normed, square[1]).reshape(length, H, DH)
    value_heads = (matmul(normed, square[2]) + small_rows[13]).reshape(length, H, DH)
    offsets = (length - 1 - jnp.arange(2 * length, dtype=jnp.int32)).astype(jnp.float32)
    position_heads = matmul(sinusoid(offsets), square[4]).reshape(2 * length, H, DH)
    content_query = (queries + small_rows[15]).reshape(block_count, block_rows, H, DH)
    position_query = (queries + small_rows[16]).reshape(block_count, block_rows, H, DH)
    first_rows = jnp.arange(block_count, dtype=jnp.int32) * block_rows
    arrays = (key_heads, value_heads, position_heads, segment, valid)
    checked = jax.checkpoint(
        lambda shared_arrays, block_item: block_scores(
            shared_arrays, block_item, length, block_rows
        )
    )
    context = lax.map(
        lambda block_item: checked(arrays, block_item), (content_query, position_query, first_rows)
    )
    return matmul(context.reshape(length, D), square[3]) + small_rows[14]


def convolution(normed, segment, valid, conv_proj, square, small_rows):
    length = normed.shape[0]
    doubled = matmul(normed, conv_proj) + jnp.concatenate([small_rows[19], small_rows[20]])
    gated = doubled[:, :D] * jax.nn.sigmoid(doubled[:, D:]) * valid.astype(jnp.float32)[:, None]
    half_kernel = (K - 1) // 2
    padded = jnp.pad(gated, ((half_kernel, half_kernel), (0, 0)))
    segment_pad = jnp.pad(segment, (half_kernel, half_kernel), constant_values=-1)
    kernel_first = 23 + 2 * (FF // D)
    mixed_rows = jnp.zeros_like(gated) + small_rows[21]
    for tap_index in range(K):
        matching = (segment_pad[tap_index : tap_index + length] == segment).astype(jnp.float32)[
            :, None
        ]
        mixed_rows = (
            mixed_rows
            + matching
            * padded[tap_index : tap_index + length]
            * small_rows[kernel_first + tap_index]
        )
    normed_inner = layer_norm(mixed_rows, small_rows[6], small_rows[7])
    return matmul(swish_unit(normed_inner), square[5]) + small_rows[22]


def conformer(inputs_pack, segment, valid, params):
    feed_in, feed_out, square, conv_proj, small_rows = params
    bias_count = FF // D
    first_bias = small_rows[23 : 23 + bias_count].reshape(FF)
    second_bias = small_rows[23 + bias_count : 23 + 2 * bias_count].reshape(FF)
    hidden = inputs_pack + 0.5 * feed_forward(
        layer_norm(inputs_pack, small_rows[0], small_rows[1]),
        feed_in[0],
        feed_out[0],
        first_bias,
        small_rows[17],
    )
    hidden = hidden + attention(
        layer_norm(hidden, small_rows[2], small_rows[3]), segment, valid, square, small_rows
    )
    hidden = hidden + convolution(
        layer_norm(hidden, small_rows[4], small_rows[5]),
        segment,
        valid,
        conv_proj,
        square,
        small_rows,
    )
    hidden = hidden + 0.5 * feed_forward(
        layer_norm(hidden, small_rows[8], small_rows[9]),
        feed_in[1],
        feed_out[1],
        second_bias,
        small_rows[18],
    )
    return layer_norm(hidden, small_rows[10], small_rows[11])


def adamw_update(weight, first, second, gradient, clip_factor, step_float, step_rate, decay_rate):
    clipped = clip_factor * gradient
    first_next = BETA_ONE * first + (1.0 - BETA_ONE) * clipped
    second_next = BETA_TWO * second + (1.0 - BETA_TWO) * clipped * clipped
    first_hat = first_next / (1.0 - jnp.power(BETA_ONE, step_float))
    second_hat = second_next / (1.0 - jnp.power(BETA_TWO, step_float))
    weight_next = weight - step_rate * (
        first_hat / (jnp.sqrt(second_hat) + ADAM_EPS) + decay_rate * weight
    )
    return (first_next, second_next, weight_next)


def pack_function(params, packed_item):
    return conformer(packed_item[0], packed_item[1], packed_item[2], params)


def local(
    inputs,
    cotangent,
    segments,
    valid_mask,
    step_count,
    feed_in,
    feed_out,
    square_proj,
    conv_proj,
    small_params,
    feed_in_first,
    feed_in_second,
    feed_out_first,
    feed_out_second,
    square_first,
    square_second,
    conv_first,
    conv_second,
    small_first,
    small_second,
):
    gathered = (
        lax.all_gather(feed_in, ("dp", "fsdp"), axis=1, tiled=True),
        lax.all_gather(feed_out, ("dp", "fsdp"), axis=1, tiled=True),
        lax.all_gather(square_proj, ("dp", "fsdp"), axis=1, tiled=True),
        lax.all_gather(conv_proj, ("dp", "fsdp"), axis=0, tiled=True),
        lax.all_gather(small_params, ("dp", "fsdp"), axis=1, tiled=True),
    )
    checked_pack = jax.checkpoint(pack_function)

    def local_layer(inputs_local, params):
        return lax.map(
            lambda packed_item: checked_pack(params, packed_item),
            (inputs_local, segments, valid_mask),
        )

    layer_rows = local_layer(inputs, gathered)
    regathered = (
        lax.all_gather(feed_in, ("dp", "fsdp"), axis=1, tiled=True),
        lax.all_gather(feed_out, ("dp", "fsdp"), axis=1, tiled=True),
        lax.all_gather(square_proj, ("dp", "fsdp"), axis=1, tiled=True),
        lax.all_gather(conv_proj, ("dp", "fsdp"), axis=0, tiled=True),
        lax.all_gather(small_params, ("dp", "fsdp"), axis=1, tiled=True),
    )
    pull_back = jax.vjp(local_layer, inputs, regathered)[1]
    input_rows, local_grads = pull_back(cotangent)
    grad_in, grad_out, grad_square, grad_conv, grad_small = local_grads
    reduced = (
        lax.psum_scatter(grad_in, ("dp", "fsdp"), scatter_dimension=1, tiled=True),
        lax.psum_scatter(grad_out, ("dp", "fsdp"), scatter_dimension=1, tiled=True),
        lax.psum_scatter(grad_square, ("dp", "fsdp"), scatter_dimension=1, tiled=True),
        lax.psum_scatter(grad_conv, ("dp", "fsdp"), scatter_dimension=0, tiled=True),
        lax.psum_scatter(grad_small, ("dp", "fsdp"), scatter_dimension=1, tiled=True),
    )
    partial_sum = sum((jnp.sum(grad_part * grad_part) for grad_part in reduced))
    gradient_norm = jnp.sqrt(lax.psum(partial_sum, ("dp", "fsdp")))
    clip_factor = jnp.minimum(1.0, CLIP_NORM / (gradient_norm + 1e-06))
    step_float = step_count[0].astype(jnp.float32)
    weights = (feed_in, feed_out, square_proj, conv_proj, small_params)
    firsts = (feed_in_first, feed_out_first, square_first, conv_first, small_first)
    seconds = (feed_in_second, feed_out_second, square_second, conv_second, small_second)
    rates = (MATRIX_RATE, MATRIX_RATE, MATRIX_RATE, MATRIX_RATE, VECTOR_RATE)
    decays = (MATRIX_DECAY, MATRIX_DECAY, MATRIX_DECAY, MATRIX_DECAY, 0.0)
    results = [
        adamw_update(
            weights[number],
            firsts[number],
            seconds[number],
            reduced[number],
            clip_factor,
            step_float,
            rates[number],
            decays[number],
        )
        for number in range(5)
    ]
    return (
        layer_rows,
        input_rows,
        gradient_norm,
        results[0][0],
        results[0][1],
        results[0][2],
        results[1][0],
        results[1][1],
        results[1][2],
        results[2][0],
        results[2][1],
        results[2][2],
        results[3][0],
        results[3][1],
        results[3][2],
        results[4][0],
        results[4][1],
        results[4][2],
    )


def solution(mesh):
    return jax.shard_map(
        local,
        mesh=mesh,
        in_specs=(
            P(("dp", "fsdp"), None, None),
            P(("dp", "fsdp"), None, None),
            P(("dp", "fsdp"), None),
            P(("dp", "fsdp"), None),
            P(),
            P(None, ("dp", "fsdp"), None),
            P(None, ("dp", "fsdp"), None),
            P(None, ("dp", "fsdp"), None),
            P(("dp", "fsdp"), None),
            P(None, ("dp", "fsdp")),
            P(None, ("dp", "fsdp"), None),
            P(None, ("dp", "fsdp"), None),
            P(None, ("dp", "fsdp"), None),
            P(None, ("dp", "fsdp"), None),
            P(None, ("dp", "fsdp"), None),
            P(None, ("dp", "fsdp"), None),
            P(("dp", "fsdp"), None),
            P(("dp", "fsdp"), None),
            P(None, ("dp", "fsdp")),
            P(None, ("dp", "fsdp")),
        ),
        out_specs=(
            P(("dp", "fsdp"), None, None),
            P(("dp", "fsdp"), None, None),
            P(),
            P(None, ("dp", "fsdp"), None),
            P(None, ("dp", "fsdp"), None),
            P(None, ("dp", "fsdp"), None),
            P(None, ("dp", "fsdp"), None),
            P(None, ("dp", "fsdp"), None),
            P(None, ("dp", "fsdp"), None),
            P(None, ("dp", "fsdp"), None),
            P(None, ("dp", "fsdp"), None),
            P(None, ("dp", "fsdp"), None),
            P(("dp", "fsdp"), None),
            P(("dp", "fsdp"), None),
            P(("dp", "fsdp"), None),
            P(None, ("dp", "fsdp")),
            P(None, ("dp", "fsdp")),
            P(None, ("dp", "fsdp")),
        ),
        check_vma=False,
    )
```

profile of v0, /device:TPU:0, one launch (start us, length us, event | category | flops | bytes accessed | tf_op | source)
XLA Modules:
  0.0 1792.2 jit_solution(8585510249538667268)
XLA Ops:
  10.1 45.1 %all_gather.20 = f32[40,512]{0,1:T(8,128)S(1)} all-gather(f32[40,16]{0,1:T(8,128)} %param.33), channel_id=1, replica_groups=mesh['dp'=4,'fsdp'=8] {'dp','fsdp'}, dimensions={1}, use_global_device_ids=true | all-gather | bytes 84480 | tf_op jit(solution)/shard_map/all_gather | solution.py:200
  55.3 28.6 %all-gather.9.cloned.1.call-done = f32[6,512,512]{2,1,0:T(8,128)} async-done(((f32[6,16,512]{2,1,0:T(8,128)}), f32[6,512,512]{2,1,0:T(8,128)}) %all-gather.9.cloned.1.call-update) | async-done | bytes 6291472 | tf_op jit(solution)/shard_map/all_gather | solution.py:198
  83.8 6.6 copy.118
  90.4 51.7 %all-gather.11.cloned.1.call-done = f32[512,1024]{1,0:T(8,128)} async-done(((f32[16,1024]{1,0:T(8,128)}), f32[512,1024]{1,0:T(8,128)}) %all-gather.11.cloned.1.call-update) | async-done | bytes 2097168 | tf_op jit(solution)/shard_map/all_gather | solution.py:199
  142.1 79.4 %all-gather.5.cloned.1.call-done = f32[2,512,2048]{2,1,0:T(8,128)} async-done(((f32[2,16,2048]{2,1,0:T(8,128)}), f32[2,512,2048]{2,1,0:T(8,128)}) %all-gather.5.cloned.1.call-update) | async-done | bytes 8388624 | tf_op jit(solution)/shard_map/all_gather | solution.py:196
  221.5 79.0 %all-gather.7.cloned.1.call-done = f32[2,2048,512]{2,1,0:T(8,128)} async-done(((f32[2,64,512]{2,1,0:T(8,128)}), f32[2,2048,512]{2,1,0:T(8,128)}) %all-gather.7.cloned.1.call-update) | async-done | bytes 8388624 | tf_op jit(solution)/shard_map/all_gather | solution.py:197
  301.6 571.2 %while.44 = (s32[]{:T(128)}, f32[2,512,2048]{2,1,0:T(8,128)}, f32[2,2048,512]{2,1,0:T(8,128)}, f32[6,512,512]{2,1,0:T(8,128)}, f32[512,1024]{1,0:T(8,128)}, /*in...) while((s32[]{:T(128)}, f32[2,512,2048]{2,1,0:T(8,128)}, ...), condition=%wide.region_81.82_spmd.clone, body=%wide.region_16.81_spmd.clone.sunk | while | flops 64936935424 | bytes 803216960 | solution.py:205
  313.9 7.7 fusion.645
  337.3 14.2 copy.184
  354.6 8.0 reshape.1150
  389.9 7.3 fusion.662
  403.7 7.0 multiply_reduce_fusion.71
  457.0 7.9 reshape.1151
  511.5 12.3 dynamic_update_slice.49
  526.4 6.6 fusion.680
  595.6 7.6 fusion.645
  618.8 14.1 copy.184
  636.0 8.0 reshape.1150
  671.4 7.3 fusion.662
  685.2 7.0 multiply_reduce_fusion.71
  738.5 7.9 reshape.1151
  792.9 12.3 dynamic_update_slice.49
  852.2 7.2 select_add_fusion.10
  888.4 117.8 %reduce-scatter.14.cloned.1.call-done = f32[40,16]{0,1:T(8,128)} async-done(((f32[40,512]{0,1:T(8,128)}), f32[40,16]{0,1:T(8,128)}) %reduce-scatter.14.cloned.1.call-update) | async-done | bytes 2576 | tf_op jit(solution)/shard_map/reduce_scatter | solution.py:226
  1007.5 133.8 %reduce-scatter.12.cloned.1.call-done = f32[16,1024]{1,0:T(8,128)} async-done(((f32[512,1024]{1,0:T(8,128)}), f32[16,1024]{1,0:T(8,128)}) %reduce-scatter.12.cloned.1.call-update) | async-done | bytes 65552 | tf_op jit(solution)/shard_map/reduce_scatter | solution.py:225
  1142.7 115.5 %reduce-scatter.10.cloned.1.call-done = f32[6,16,512]{2,1,0:T(8,128)} async-done(((f32[6,512,512]{2,1,0:T(8,128)}), f32[6,16,512]{2,1,0:T(8,128)}) %reduce-scatter.10.cloned.1.call-update) | async-done | bytes 196624 | tf_op jit(solution)/shard_map/reduce_scatter | solution.py:224
  1259.8 151.7 %reduce-scatter.6.cloned.1.call-done = f32[2,16,2048]{2,1,0:T(8,128)} async-done(((f32[2,512,2048]{2,1,0:T(8,128)}), f32[2,16,2048]{2,1,0:T(8,128)}) %reduce-scatter.6.cloned.1.call-update) | async-done | bytes 262160 | tf_op jit(solution)/shard_map/reduce_scatter | solution.py:222
  1413.2 150.5 %reduce-scatter.8.cloned.1.call-done = f32[2,64,512]{2,1,0:T(8,128)} async-done(((f32[2,2048,512]{2,1,0:T(8,128)}), f32[2,64,512]{2,1,0:T(8,128)}) %reduce-scatter.8.cloned.1.call-update) | async-done | bytes 262160 | tf_op jit(solution)/shard_map/reduce_scatter | solution.py:223
  1569.7 168.7 %while.43 = (s32[]{:T(128)}, f32[2,256,512]{2,1,0:T(8,128)}, f32[2,256,512]{2,1,0:T(8,128)S(1)}, f32[40,512]{1,0:T(8,128)S(1)}, f32[2,512,2048]{2,1,0:T(8,128)},...) while((s32[]{:T(128)}, f32[2,256,512]{2,1,0:T(8,128)}, ...), condition=%wide.region_15.16_spmd, body=%wide.region_0.15_spmd.sunk | while | flops 20156383232 | bytes 220463152 | solution.py:205
  1610.5 8.0 reshape.1149
  1693.8 8.0 reshape.1149
  1738.5 36.9 %psum.7 = f32[]{:T(128)} all-reduce(f32[]{:T(128)S(6)} %add.1779), channel_id=1, replica_groups=mesh['dp'=4,'fsdp'=8] {'dp','fsdp'}, use_global_device_ids=true, to_apply=%region_92.93 | all-reduce | flops 1 | bytes 8 | tf_op jit(solution)/shard_map/psum | solution.py:229
  (973 shorter events, 601.7 us)
Async XLA Ops:
  7.2 76.6 %all-gather.9.cloned.1.call-start = ((), (), s32[]{:S(2)}) async-start(), calls=%async_computation.7 | async-start | bytes 6488064 | tf_op jit(solution)/shard_map/all_gather | solution.py:198
  7.9 134.2 %all-gather.11.cloned.1.call-start = ((), (), s32[]{:S(2)}) async-start(), calls=%async_computation.8 | async-start | bytes 2162688 | tf_op jit(solution)/shard_map/all_gather | solution.py:199
  8.7 212.8 %all-gather.5.cloned.1.call-start = ((), (), s32[]{:S(2)}) async-start(), calls=%async_computation.5 | async-start | bytes 8650752 | tf_op jit(solution)/shard_map/all_gather | solution.py:196
  9.4 291.1 %all-gather.7.cloned.1.call-start = ((), (), s32[]{:S(2)}) async-start(), calls=%async_computation.6 | async-start | bytes 8650752 | tf_op jit(solution)/shard_map/all_gather | solution.py:197
  10.0 996.2 %reduce-scatter.14.cloned.1.call-start = ((), (), s32[]{:S(2)}) async-start(), calls=%async_computation.13 | async-start | bytes 270336 | tf_op jit(solution)/shard_map/reduce_scatter | solution.py:226
  55.2 35.3 %copy-start.62 = (f32[40,512]{0,1:T(8,128)}, f32[40,512]{0,1:T(8,128)S(1)}, u32[]{:S(2)}) copy-start(f32[40,512]{0,1:T(8,128)S(1)} %all_gather.20) | copy-start | bytes 245764
  55.3 246.3 %copy-start.32 = (f32[2,256,512]{2,1,0:T(8,128)S(1)}, f32[2,256,512]{2,1,0:T(8,128)}, u32[]{:S(2)}) copy-start(f32[2,256,512]{2,1,0:T(8,128)} %param.24) | copy-start | bytes 3145732
  308.1 74.9 %copy-start.87 = (f32[1,512]{1,0:T(1,128)}, f32[1,512]{1,0:T(1,128)S(1)}, u32[]{:S(2)}) copy-start(f32[1,512]{1,0:T(1,128)S(1)} %get-tuple-element.1690) | copy-start | bytes 6148 | tf_op jit(solution)/shard_map/transpose(jvp())/while
  308.1 74.9 %copy-start.120 = (f32[1,512]{1,0:T(1,128)}, f32[1,512]{1,0:T(1,128)S(1)}, u32[]{:S(2)}) copy-start(f32[1,512]{1,0:T(1,128)S(1)} %get-tuple-element.1691) | copy-start | bytes 6148 | tf_op jit(solution)/shard_map/transpose(jvp())/while
  327.9 40.7 %copy-start.15 = (f32[256,512]{0,1:T(8,128)}, f32[256,512]{0,1:T(8,128)S(1)}, u32[]{:S(2)}) copy-start(f32[256,512]{0,1:T(8,128)S(1)} %copy.182) | copy-start | bytes 1572868 | tf_op jit(solution)/shard_map/transpose(jvp())/while
  331.8 36.8 %copy-start.17 = (f32[256,8,64]{0,2,1:T(8,128)}, f32[256,8,64]{0,2,1:T(8,128)S(1)}, u32[]{:S(2)}) copy-start(f32[256,8,64]{0,2,1:T(8,128)S(1)} %fusion.648) | copy-start | bytes 1572868 | tf_op jit(solution)/shard_map/transpose(jvp())/while
  333.7 113.7 %copy-start.5 = (f32[512,8,64]{0,2,1:T(8,128)}, f32[512,8,64]{0,2,1:T(8,128)S(1)}, u32[]{:S(2)}) copy-start(f32[512,8,64]{0,2,1:T(8,128)S(1)} %fusion.649) | copy-start | bytes 3145732 | tf_op jit(solution)/shard_map/transpose(jvp())/while
  589.8 74.7 %copy-start.87 = (f32[1,512]{1,0:T(1,128)}, f32[1,512]{1,0:T(1,128)S(1)}, u32[]{:S(2)}) copy-start(f32[1,512]{1,0:T(1,128)S(1)} %get-tuple-element.1690) | copy-start | bytes 6148 | tf_op jit(solution)/shard_map/transpose(jvp())/while
  589.8 74.7 %copy-start.120 = (f32[1,512]{1,0:T(1,128)}, f32[1,512]{1,0:T(1,128)S(1)}, u32[]{:S(2)}) copy-start(f32[1,512]{1,0:T(1,128)S(1)} %get-tuple-element.1691) | copy-start | bytes 6148 | tf_op jit(solution)/shard_map/transpose(jvp())/while
  609.4 40.6 %copy-start.15 = (f32[256,512]{0,1:T(8,128)}, f32[256,512]{0,1:T(8,128)S(1)}, u32[]{:S(2)}) copy-start(f32[256,512]{0,1:T(8,128)S(1)} %copy.182) | copy-start | bytes 1572868 | tf_op jit(solution)/shard_map/transpose(jvp())/while
  613.3 36.7 %copy-start.17 = (f32[256,8,64]{0,2,1:T(8,128)}, f32[256,8,64]{0,2,1:T(8,128)S(1)}, u32[]{:S(2)}) copy-start(f32[256,8,64]{0,2,1:T(8,128)S(1)} %fusion.648) | copy-start | bytes 1572868 | tf_op jit(solution)/shard_map/transpose(jvp())/while
  615.3 113.6 %copy-start.5 = (f32[512,8,64]{0,2,1:T(8,128)}, f32[512,8,64]{0,2,1:T(8,128)S(1)}, u32[]{:S(2)}) copy-start(f32[512,8,64]{0,2,1:T(8,128)S(1)} %fusion.649) | copy-start | bytes 3145732 | tf_op jit(solution)/shard_map/transpose(jvp())/while
  873.6 267.6 %reduce-scatter.12.cloned.1.call-start = ((), (), s32[]{:S(2)}) async-start(), calls=%async_computation.12 | async-start | bytes 2162688 | tf_op jit(solution)/shard_map/reduce_scatter | solution.py:225
  874.2 384.0 %reduce-scatter.10.cloned.1.call-start = ((), (), s32[]{:S(2)}) async-start(), calls=%async_computation.11 | async-start | bytes 6488064 | tf_op jit(solution)/shard_map/reduce_scatter | solution.py:224
  875.0 536.6 %reduce-scatter.6.cloned.1.call-start = ((), (), s32[]{:S(2)}) async-start(), calls=%async_computation.9 | async-start | bytes 8650752 | tf_op jit(solution)/shard_map/reduce_scatter | solution.py:222
  875.7 688.0 %reduce-scatter.8.cloned.1.call-start = ((), (), s32[]{:S(2)}) async-start(), calls=%async_computation.10 | async-start | bytes 8650752 | tf_op jit(solution)/shard_map/reduce_scatter | solution.py:223
  883.8 685.9 %copy-start.4 = (f32[512,1024]{1,0:T(8,128)S(1)}, f32[512,1024]{1,0:T(8,128)}, u32[]{:S(2)}) copy-start(f32[512,1024]{1,0:T(8,128)} %get-tuple-element.1927) | copy-start | bytes 6291460
  883.8 685.9 %copy-start.34 = (f32[2,256,512]{2,1,0:T(8,128)S(1)}, f32[2,256,512]{2,1,0:T(8,128)}, u32[]{:S(2)}) copy-start(f32[2,256,512]{2,1,0:T(8,128)} %param.24) | copy-start | bytes 3145732
  1569.7 211.5 %copy-start.68 = (f32[2,16,2048]{2,1,0:T(8,128)S(1)}, f32[2,16,2048]{2,1,0:T(8,128)}, u32[]{:S(2)}) copy-start(f32[2,16,2048]{2,1,0:T(8,128)} %param.29) | copy-start | bytes 786436
  1574.5 15.5 copy-start.72
  1574.5 15.5 copy-start.73
  1657.6 15.5 copy-start.72
  1657.6 15.5 copy-start.73
  1738.4 44.9 %copy-start.69 = (f32[2,64,512]{2,1,0:T(8,128)S(1)}, f32[2,64,512]{2,1,0:T(8,128)}, u32[]{:S(2)}) copy-start(f32[2,64,512]{2,1,0:T(8,128)} %param.30) | copy-start | bytes 786436
  1738.4 44.9 %copy-start.70 = (f32[2,64,512]{2,1,0:T(8,128)S(1)}, f32[2,64,512]{2,1,0:T(8,128)}, u32[]{:S(2)}) copy-start(f32[2,64,512]{2,1,0:T(8,128)} %reduce-scatter.8.cloned.1.call-done) | copy-start | bytes 786436
  1738.4 44.9 %copy-start.76 = (f32[2,64,512]{2,1,0:T(8,128)S(1)}, f32[2,64,512]{2,1,0:T(8,128)}, u32[]{:S(2)}) copy-start(f32[2,64,512]{2,1,0:T(8,128)} %param.37) | copy-start | bytes 786436
  1738.4 44.9 %copy-start.77 = (f32[2,64,512]{2,1,0:T(8,128)S(1)}, f32[2,64,512]{2,1,0:T(8,128)}, u32[]{:S(2)}) copy-start(f32[2,64,512]{2,1,0:T(8,128)} %param.36) | copy-start | bytes 786436
  (241 other events, 980.2 us)
Sparse Core Ops, SparseCore 0:
  11.0 72.7 all-gather.8
  86.8 55.2 all-gather.10
  145.2 76.2 all-gather.4
  224.4 76.0 all-gather.6
  873.8 132.3 reduce-scatter.13
  1008.4 132.8 reduce-scatter.11
  1146.9 111.3 reduce-scatter.9
  1260.6 150.8 reduce-scatter.5
  1414.0 149.7 reduce-scatter.7
where the time goes:
time: 1800 us; the launch traced here: 1790 us
  waiting for transfers between devices  913 us (51%)
  matrix products  409 us (23%)
  local copies, waits for them, and re-layouts  266 us (15%)
  other arithmetic  86.4 us (5%)
  blocking collectives  82 us (5%)
  between operations  20 us (1%)
    dot_general x85, matrix products, matmul(): jnp.dot(left, right, precision=PRECISE, preferred_element_type=jnp.float32)  312 us
    reduce_scatter x1, waiting for transfers between devices, local(): lax.psum_scatter(grad_in, ('dp', 'fsdp'), scatter_dimension=1, tiled=True)  152 us
    reduce_scatter x1, waiting for transfers between devices, local(): lax.psum_scatter(grad_out, ('dp', 'fsdp'), scatter_dimension=1, tiled=True)  151 us
    reduce_scatter x1, waiting for transfers between devices, local(): lax.psum_scatter(grad_conv, ('dp', 'fsdp'), scatter_dimension=0, tiled=True)  134 us
    reduce_scatter x1, waiting for transfers between devices, local(): lax.psum_scatter(grad_small, ('dp', 'fsdp'), scatter_dimension=1, tiled=T...  118 us
    reduce_scatter x1, waiting for transfers between devices, local(): lax.psum_scatter(grad_square, ('dp', 'fsdp'), scatter_dimension=1, tiled=...  116 us
    while x530, local copies, waits for them, and re-layouts  88.7 us
    all_gather x1, waiting for transfers between devices, local(): lax.all_gather(feed_in, ('dp', 'fsdp'), axis=1, tiled=True)  79.4 us
  transfers between devices with their start and end apart: 9, of which 9 were waited for; matrix products, arithmetic and copies ran while one was open for 1% of the time, Pallas kernels for 0%

commit v1 on v0

v1 whole, which is shorter than its diff:
```python
import functools
import math

import jax
import jax.numpy as jnp
import numpy as np
from jax import lax
from jax.experimental import pallas as pl
from jax.experimental.pallas import tpu as pltpu
from jax.sharding import PartitionSpec as P

D = 512
H = 8
DH = 64
FF = 2048
K = 9
NC = FF // D
TAP = 23 + 2 * NC
NORM_EPS = 1e-05
BETA_ONE = 0.9
BETA_TWO = 0.999
ADAM_EPS = 1e-08
CLIP_NORM = 1.0
MATRIX_RATE = 0.03
VECTOR_RATE = 0.4
MATRIX_DECAY = 0.01
VMEM_LIMIT = 60 * 2**20

f32 = jnp.float32
bf16 = jnp.bfloat16
NN = (((1,), (0,)), ((), ()))
NT = (((1,), (1,)), ((), ()))
TN = (((0,), (0,)), ((), ()))


def split(value):
    high = value.astype(bf16)
    return high, (value - high.astype(f32)).astype(bf16)


def dot(left, right, dims):
    return lax.dot_general(left, right, dims, preferred_element_type=f32)


def dot3(left, right, dims):
    return dot(left[0], right[0], dims) + (dot(left[0], right[1], dims) + dot(left[1], right[0], dims))


def normalize(values):
    centred = values - jnp.mean(values, axis=-1, keepdims=True)
    inverse = lax.rsqrt(jnp.mean(centred * centred, axis=-1, keepdims=True) + NORM_EPS)
    return centred * inverse, inverse


def normalize_back(scaled, xhat, inverse):
    return (scaled - jnp.mean(scaled, axis=-1, keepdims=True) - xhat * jnp.mean(scaled * xhat, axis=-1, keepdims=True)) * inverse


def column_sum(values):
    return jnp.sum(values, axis=0, keepdims=True)


def row(rows_ref, index):
    return rows_ref[pl.ds(index, 1), :]


def store_split(pair_ref, value):
    high, low = split(value)
    pair_ref[0] = high
    pair_ref[1] = low


def load_split(pair_ref, *index):
    if index:
        return pair_ref[(0,) + index], pair_ref[(1,) + index]
    return pair_ref[0], pair_ref[1]


def ffn_forward_chunk(normed, u_ref, win, wout, bias):
    u = dot3(normed, split(win), NN) + bias
    u_ref[...] = u
    return dot3(split(u * jax.nn.sigmoid(u)), split(wout), NN)


def ffn_backward_chunk(normed, u, df, win, wout):
    sig = jax.nn.sigmoid(u)
    dwout = dot3(split(u * sig), df, TN)
    du = dot3(df, split(wout), NT) * (sig * (1.0 + u * (1.0 - sig)))
    du_split = split(du)
    dwin = dot3(normed, du_split, TN)
    return dwin, dwout, column_sum(du), dot3(du_split, split(win), NT)


def ffn1_forward_kernel(x_ref, win_ref, wout_ref, s_ref, a1_ref, u_ref, normed):
    chunk = pl.program_id(0)

    @pl.when(chunk == 0)
    def _():
        xhat, _ = normalize(x_ref[...])
        store_split(normed, xhat * s_ref[0:1] + s_ref[1:2])
        a1_ref[...] = x_ref[...] + 0.5 * s_ref[17:18]

    out = ffn_forward_chunk(load_split(normed), u_ref, win_ref[...], wout_ref[...], row(s_ref, 23 + chunk))
    a1_ref[...] += 0.5 * out


def ffn1_forward(x, win, wout, s):
    frames = x.shape[0]
    whole = pl.BlockSpec((frames, D), lambda c: (0, 0))
    return pl.pallas_call(
        ffn1_forward_kernel,
        grid=(NC,),
        in_specs=[
            whole,
            pl.BlockSpec((D, D), lambda c: (0, c)),
            pl.BlockSpec((D, D), lambda c: (c, 0)),
            pl.BlockSpec(s.shape, lambda c: (0, 0)),
        ],
        out_specs=[whole, pl.BlockSpec((frames, D), lambda c: (0, c))],
        out_shape=[jax.ShapeDtypeStruct((frames, D), f32), jax.ShapeDtypeStruct((frames, FF), f32)],
        scratch_shapes=[pltpu.VMEM((2, frames, D), bf16)],
        compiler_params=pltpu.CompilerParams(vmem_limit_bytes=VMEM_LIMIT),
        name="ffn1_forward",
    )(x, win, wout, s)


def ffn1_backward_kernel(da_ref, x_ref, u_ref, win_ref, wout_ref, s_ref, dx_ref, dwin_ref, dwout_ref, ds_ref, normed, df):
    chunk = pl.program_id(0)

    @pl.when(chunk == 0)
    def _():
        xhat, _ = normalize(x_ref[...])
        store_split(normed, xhat * s_ref[0:1] + s_ref[1:2])
        half = 0.5 * da_ref[...]
        store_split(df, half)
        ds_ref[...] = jnp.zeros_like(ds_ref)
        ds_ref[2:3] = column_sum(half)
        dx_ref[...] = jnp.zeros_like(dx_ref)

    dwin, dwout, dbias, dnormed = ffn_backward_chunk(load_split(normed), u_ref[...], load_split(df), win_ref[...], wout_ref[...])
    dwin_ref[...] = dwin
    dwout_ref[...] = dwout
    ds_ref[pl.ds(4 + chunk, 1), :] = dbias
    dx_ref[...] += dnormed

    @pl.when(chunk == NC - 1)
    def _():
        xhat, inverse = normalize(x_ref[...])
        dn = dx_ref[...]
        ds_ref[0:1] = column_sum(dn * xhat)
        ds_ref[1:2] = column_sum(dn)
        dx_ref[...] = da_ref[...] + normalize_back(dn * s_ref[0:1], xhat, inverse)


def ffn1_backward(da, x, u, win, wout, s):
    frames = x.shape[0]
    whole = pl.BlockSpec((frames, D), lambda c: (0, 0))
    across = pl.BlockSpec((D, D), lambda c: (0, c))
    down = pl.BlockSpec((D, D), lambda c: (c, 0))
    return pl.pallas_call(
        ffn1_backward_kernel,
        grid=(NC,),
        in_specs=[whole, whole, pl.BlockSpec((frames, D), lambda c: (0, c)), across, down, pl.BlockSpec(s.shape, lambda c: (0, 0))],
        out_specs=[whole, across, down, pl.BlockSpec((8, D), lambda c: (0, 0))],
        out_shape=[
            jax.ShapeDtypeStruct((frames, D), f32),
            jax.ShapeDtypeStruct((D, FF), f32),
            jax.ShapeDtypeStruct((FF, D), f32),
            jax.ShapeDtypeStruct((8, D), f32),
        ],
        scratch_shapes=[pltpu.VMEM((2, frames, D), bf16), pltpu.VMEM((2, frames, D), bf16)],
        compiler_params=pltpu.CompilerParams(vmem_limit_bytes=VMEM_LIMIT),
        name="ffn1_backward",
    )(da, x, u, win, wout, s)


def ffn2_kernel(a3_ref, cot_ref, win_ref, wout_ref, s_ref, out_ref, da3_ref, dwin_ref, dwout_ref, ds_ref, normed, df, hidden, da4):
    step = pl.program_id(0)

    @pl.when(step == 0)
    def _():
        xhat, _ = normalize(a3_ref[...])
        store_split(normed, xhat * s_ref[8:9] + s_ref[9:10])
        da4[...] = a3_ref[...] + 0.5 * s_ref[18:19]

    @pl.when(step < NC)
    def _():
        out = ffn_forward_chunk(load_split(normed), hidden.at[step], win_ref[...], wout_ref[...], row(s_ref, 23 + NC + step))
        da4[...] += 0.5 * out

    @pl.when(step == NC - 1)
    def _():
        xhat, inverse = normalize(da4[...])
        out_ref[...] = xhat * s_ref[10:11] + s_ref[11:12]
        cot = cot_ref[...]
        ds_ref[...] = jnp.zeros_like(ds_ref)
        ds_ref[8:9] = column_sum(cot * xhat)
        ds_ref[9:10] = column_sum(cot)
        grad = normalize_back(cot * s_ref[10:11], xhat, inverse)
        da4[...] = grad
        half = 0.5 * grad
        store_split(df, half)
        ds_ref[2:3] = column_sum(half)
        da3_ref[...] = jnp.zeros_like(da3_ref)

    @pl.when(step >= NC)
    def _():
        dwin, dwout, dbias, dnormed = ffn_backward_chunk(load_split(normed), hidden[step - NC], load_split(df), win_ref[...], wout_ref[...])
        dwin_ref[...] = dwin
        dwout_ref[...] = dwout
        ds_ref[pl.ds(4 + step - NC, 1), :] = dbias
        da3_ref[...] += dnormed

    @pl.when(step == 2 * NC - 1)
    def _():
        xhat, inverse = normalize(a3_ref[...])
        dn = da3_ref[...]
        ds_ref[0:1] = column_sum(dn * xhat)
        ds_ref[1:2] = column_sum(dn)
        da3_ref[...] = da4[...] + normalize_back(dn * s_ref[8:9], xhat, inverse)


def ffn2(a3, cot, win, wout, s):
    frames = a3.shape[0]
    whole = pl.BlockSpec((frames, D), lambda c: (0, 0))
    return pl.pallas_call(
        ffn2_kernel,
        grid=(2 * NC,),
        in_specs=[
            whole,
            whole,
            pl.BlockSpec((D, D), lambda c: (0, lax.rem(c, NC))),
            pl.BlockSpec((D, D), lambda c: (lax.rem(c, NC), 0)),
            pl.BlockSpec(s.shape, lambda c: (0, 0)),
        ],
        out_specs=[
            whole,
            whole,
            pl.BlockSpec((D, D), lambda c: (0, jnp.maximum(c - NC, 0))),
            pl.BlockSpec((D, D), lambda c: (jnp.maximum(c - NC, 0), 0)),
            pl.BlockSpec((16, D), lambda c: (0, 0)),
        ],
        out_shape=[
            jax.ShapeDtypeStruct((frames, D), f32),
            jax.ShapeDtypeStruct((frames, D), f32),
            jax.ShapeDtypeStruct((D, FF), f32),
            jax.ShapeDtypeStruct((FF, D), f32),
            jax.ShapeDtypeStruct((16, D), f32),
        ],
        scratch_shapes=[
            pltpu.VMEM((2, frames, D), bf16),
            pltpu.VMEM((2, frames, D), bf16),
            pltpu.VMEM((NC, frames, D), f32),
            pltpu.VMEM((frames, D), f32),
        ],
        compiler_params=pltpu.CompilerParams(vmem_limit_bytes=VMEM_LIMIT),
        name="ffn2",
    )(a3, cot, win, wout, s)


def sinusoid_table(length):
    offsets = length // 2 - np.arange(length, dtype=np.float64)
    frequency = 10000.0 ** (-2.0 * np.arange(D // 2, dtype=np.float64) / D)
    angles = offsets[:, None] * frequency[None, :]
    table = np.concatenate([np.sin(angles), np.cos(angles)], axis=1).astype(np.float32)
    return np.stack([table, table[::-1]])


def shift_rows(scores):
    return pltpu.roll(scores, scores.shape[1] // 2, 1, stride=1, stride_axis=0)


def pair_masks():
    lane = lax.broadcasted_iota(jnp.int32, (1, 2 * DH), 1)
    first = (lane < DH).astype(f32)
    return first, 1.0 - first


def attention_forward_kernel(length, a1_ref, w_ref, pe_ref, s_ref, segcol_ref, keyrow_ref, a2_ref, qkv_ref, rel_ref, probs_ref, ctx_ref, bias):
    packs = a1_ref.shape[0] // length
    xhat, _ = normalize(a1_ref[...])
    normed = split(xhat * s_ref[2:3] + s_ref[3:4])
    qkv_ref[0] = dot3(normed, split(w_ref[0]), NN) + s_ref[12:13]
    qkv_ref[1] = dot3(normed, split(w_ref[1]), NN)
    qkv_ref[2] = dot3(normed, split(w_ref[2]), NN) + s_ref[13:14]
    rel_ref[...] = dot3(split(pe_ref[0]), split(w_ref[4]), NN)
    query = lax.broadcasted_iota(jnp.int32, (length, length), 0)
    key = lax.broadcasted_iota(jnp.int32, (length, length), 1)
    for pack in range(packs):
        same = segcol_ref[pl.ds(pack * length, length), 0:1] == keyrow_ref[pack : pack + 1, 0:length]
        bias[pack] = jnp.where(same | (query == key), 0.0, -1e30)
    first, second = pair_masks()

    def heads(item, carry):
        pack, pair = item // (H // 2), item % (H // 2)
        frames = pl.ds(pl.multiple_of(pack * length, length), length)
        lanes = pl.ds(pl.multiple_of(pair * 2 * DH, 2 * DH), 2 * DH)
        q = qkv_ref[0, frames, lanes]
        content = q + s_ref[15:16, lanes]
        position = q + s_ref[16:17, lanes]
        k = split(qkv_ref[1, frames, lanes])
        v = split(qkv_ref[2, frames, lanes])
        rel = split(rel_ref[:, lanes])
        total = jnp.zeros_like(q)
        for index, mask in enumerate((first, second)):
            scores = dot3(split(content * mask), k, NT) + shift_rows(dot3(split(position * mask), rel, NT))
            scores = scores * (1.0 / math.sqrt(DH)) + bias[pack]
            weights = jnp.exp(scores - jnp.max(scores, axis=-1, keepdims=True))
            weights = weights / jnp.sum(weights, axis=-1, keepdims=True)
            probs_ref[item * 2 + index] = weights
            total = total + dot3(split(weights), v, NN) * mask
        ctx_ref[frames, lanes] = total
        return carry

    lax.fori_loop(0, packs * (H // 2), heads, 0)
    a2_ref[...] = a1_ref[...] + dot3(split(ctx_ref[...]), split(w_ref[3]), NN) + s_ref[14:15]


def attention_forward(length, a1, square, pe, s, segcol, keyrow):
    frames = a1.shape[0]
    packs = frames // length
    vmem = pl.BlockSpec(memory_space=pltpu.VMEM)
    return pl.pallas_call(
        functools.partial(attention_forward_kernel, length),
        in_specs=[vmem] * 6,
        out_specs=[vmem] * 5,
        out_shape=[
            jax.ShapeDtypeStruct((frames, D), f32),
            jax.ShapeDtypeStruct((3, frames, D), f32),
            jax.ShapeDtypeStruct((length, D), f32),
            jax.ShapeDtypeStruct((packs * H, length, length), f32),
            jax.ShapeDtypeStruct((frames, D), f32),
        ],
        scratch_shapes=[pltpu.VMEM((packs, length, length), f32)],
        compiler_params=pltpu.CompilerParams(vmem_limit_bytes=VMEM_LIMIT),
        name="attention_forward",
    )(a1, square, pe, s, segcol, keyrow)


def attention_backward_kernel(
    length, da2_ref, a1_ref, qkv_ref, rel_ref, probs_ref, ctx_ref, w_ref, pe_ref, s_ref, da1_ref, dw_ref, ds_ref, dctx, dqkv, drel, relback, du, dv
):
    packs = a1_ref.shape[0] // length
    row_index = lax.broadcasted_iota(jnp.int32, (length, length), 0)
    lane_index = lax.broadcasted_iota(jnp.int32, (length, length), 1)
    flip = (row_index + lane_index == length - 1).astype(bf16)
    da2 = da2_ref[...]
    da2_split = split(da2)
    ds_ref[...] = jnp.zeros_like(ds_ref)
    ds_ref[2:3] = column_sum(da2)
    dw_ref[3] = dot3(split(ctx_ref[...]), da2_split, TN)
    dctx[...] = dot3(da2_split, split(w_ref[3]), NT)
    rel_split = split(rel_ref[...])
    relback[...] = dot(flip, rel_split[0], NN) + dot(flip, rel_split[1], NN)
    drel[...] = jnp.zeros_like(drel)
    du[...] = jnp.zeros_like(du)
    dv[...] = jnp.zeros_like(dv)
    first, second = pair_masks()

    def heads(item, carry):
        pack, pair = item // (H // 2), item % (H // 2)
        frames = pl.ds(pl.multiple_of(pack * length, length), length)
        lanes = pl.ds(pl.multiple_of(pair * 2 * DH, 2 * DH), 2 * DH)
        q = qkv_ref[0, frames, lanes]
        content = q + s_ref[15:16, lanes]
        position = q + s_ref[16:17, lanes]
        k = qkv_ref[1, frames, lanes]
        v = split(qkv_ref[2, frames, lanes])
        rel = relback[:, lanes]
        dc = dctx[frames, lanes]
        dcontent = jnp.zeros_like(q)
        dposition = jnp.zeros_like(q)
        dkey = jnp.zeros_like(q)
        dvalue = jnp.zeros_like(q)
        drelation = jnp.zeros_like(rel)
        for index, mask in enumerate((first, second)):
            weights = probs_ref[item * 2 + index]
            dc_split = split(dc * mask)
            dvalue = dvalue + dot3(split(weights), dc_split, TN)
            dweights = dot3(dc_split, v, NT)
            dscores = weights * (dweights - jnp.sum(weights * dweights, axis=-1, keepdims=True)) * (1.0 / math.sqrt(DH))
            ds_split = split(dscores)
            dcontent = dcontent + dot3(ds_split, split(k * mask), NN)
            dkey = dkey + dot3(ds_split, split(content * mask), TN)
            shifted = split(shift_rows(dot(ds_split[0], flip, NN) + dot(ds_split[1], flip, NN)))
            dposition = dposition + dot3(shifted, split(rel * mask), NN)
            drelation = drelation + dot3(shifted, split(position * mask), TN)
        dqkv[0, frames, lanes] = dcontent + dposition
        dqkv[1, frames, lanes] = dkey
        dqkv[2, frames, lanes] = dvalue
        drel[:, lanes] += drelation
        du[0:1, lanes] += column_sum(dcontent)
        dv[0:1, lanes] += column_sum(dposition)
        return carry

    lax.fori_loop(0, packs * (H // 2), heads, 0)
    ds_ref[3:4] = du[0:1]
    ds_ref[4:5] = dv[0:1]
    ds_ref[5:6] = column_sum(dqkv[0])
    ds_ref[6:7] = column_sum(dqkv[2])
    xhat, inverse = normalize(a1_ref[...])
    normed = split(xhat * s_ref[2:3] + s_ref[3:4])
    dnormed = jnp.zeros_like(xhat)
    for index in range(3):
        grad = split(dqkv[index])
        dw_ref[index] = dot3(normed, grad, TN)
        dnormed = dnormed + dot3(grad, split(w_ref[index]), NT)
    dw_ref[4] = dot3(split(pe_ref[1]), split(drel[...]), TN)
    ds_ref[0:1] = column_sum(dnormed * xhat)
    ds_ref[1:2] = column_sum(dnormed)
    da1_ref[...] = da2_ref[...] + normalize_back(dnormed * s_ref[2:3], xhat, inverse)


def attention_backward(length, da2, a1, qkv, rel, probs, ctx, square, pe, s):
    frames = a1.shape[0]
    vmem = pl.BlockSpec(memory_space=pltpu.VMEM)
    return pl.pallas_call(
        functools.partial(attention_backward_kernel, length),
        in_specs=[vmem] * 9,
        out_specs=[vmem] * 3,
        out_shape=[
            jax.ShapeDtypeStruct((frames, D), f32),
            jax.ShapeDtypeStruct((5, D, D), f32),
            jax.ShapeDtypeStruct((8, D), f32),
        ],
        scratch_shapes=[
            pltpu.VMEM((frames, D), f32),
            pltpu.VMEM((3, frames, D), f32),
            pltpu.VMEM((length, D), f32),
            pltpu.VMEM((length, D), f32),
            pltpu.VMEM((8, D), f32),
            pltpu.VMEM((8, D), f32),
        ],
        compiler_params=pltpu.CompilerParams(vmem_limit_bytes=VMEM_LIMIT),
        name="attention_backward",
    )(da2, a1, qkv, rel, probs, ctx, square, pe, s)


EDGE = 8
HALF = (K - 1) // 2
STRIP = 64


def convolution_forward_kernel(a2_ref, proj_ref, w_ref, s_ref, match_ref, a3_ref, u_ref, mixed_ref, padded):
    frames = a2_ref.shape[0]
    xhat, _ = normalize(a2_ref[...])
    normed = split(xhat * s_ref[4:5] + s_ref[5:6])
    u_ref[:, :D] = dot3(normed, split(proj_ref[:, :D]), NN) + s_ref[19:20]
    u_ref[:, D:] = dot3(normed, split(proj_ref[:, D:]), NN) + s_ref[20:21]
    padded[0:EDGE] = jnp.zeros((EDGE, D), f32)
    padded[EDGE + frames :] = jnp.zeros((EDGE, D), f32)
    padded[EDGE : EDGE + frames] = u_ref[:, :D] * jax.nn.sigmoid(u_ref[:, D:]) * match_ref[:, K : K + 1]
    for base in range(0, frames, STRIP):
        total = jnp.zeros((STRIP, D), f32) + s_ref[21:22]
        for tap in range(K):
            source = padded[base + EDGE + tap - HALF : base + EDGE + tap - HALF + STRIP]
            total = total + match_ref[base : base + STRIP, tap : tap + 1] * source * s_ref[TAP + tap : TAP + tap + 1]
        mixed_ref[base : base + STRIP] = total
    inner, _ = normalize(mixed_ref[...])
    inner = inner * s_ref[6:7] + s_ref[7:8]
    a3_ref[...] = a2_ref[...] + dot3(split(inner * jax.nn.sigmoid(inner)), split(w_ref[...]), NN) + s_ref[22:23]


def convolution_forward(a2, proj, weight, s, match):
    frames = a2.shape[0]
    vmem = pl.BlockSpec(memory_space=pltpu.VMEM)
    return pl.pallas_call(
        convolution_forward_kernel,
        in_specs=[vmem] * 5,
        out_specs=[vmem] * 3,
        out_shape=[
            jax.ShapeDtypeStruct((frames, D), f32),
            jax.ShapeDtypeStruct((frames, 2 * D), f32),
            jax.ShapeDtypeStruct((frames, D), f32),
        ],
        scratch_shapes=[pltpu.VMEM((frames + 2 * EDGE, D), f32)],
        compiler_params=pltpu.CompilerParams(vmem_limit_bytes=VMEM_LIMIT),
        name="convolution_forward",
    )(a2, proj, weight, s, match)


def convolution_backward_kernel(
    da3_ref, a2_ref, u_ref, mixed_ref, proj_ref, w_ref, s_ref, match_ref, da2_ref, dproj_ref, dw_ref, ds_ref, padded, dpadded, dgated
):
    frames = a2_ref.shape[0]
    da3 = da3_ref[...]
    da3_split = split(da3)
    ds_ref[...] = jnp.zeros_like(ds_ref)
    ds_ref[2:3] = column_sum(da3)
    hat, inverse = normalize(mixed_ref[...])
    inner = hat * s_ref[6:7] + s_ref[7:8]
    sig = jax.nn.sigmoid(inner)
    dw_ref[...] = dot3(split(inner * sig), da3_split, TN)
    dinner = dot3(da3_split, split(w_ref[...]), NT) * (sig * (1.0 + inner * (1.0 - sig)))
    ds_ref[3:4] = column_sum(dinner * hat)
    ds_ref[4:5] = column_sum(dinner)
    dmixed = normalize_back(dinner * s_ref[6:7], hat, inverse)
    ds_ref[5:6] = column_sum(dmixed)
    zeros = jnp.zeros((EDGE, D), f32)
    padded[0:EDGE] = zeros
    padded[EDGE + frames :] = zeros
    padded[EDGE : EDGE + frames] = u_ref[:, :D] * jax.nn.sigmoid(u_ref[:, D:]) * match_ref[:, K : K + 1]
    dpadded[0:EDGE] = zeros
    dpadded[EDGE + frames :] = zeros
    dpadded[EDGE : EDGE + frames] = dmixed
    for base in range(0, frames, STRIP):
        total = jnp.zeros((STRIP, D), f32)
        center = dpadded[base + EDGE : base + EDGE + STRIP]
        for tap in range(K):
            rows = slice(base + EDGE + tap - HALF, base + EDGE + tap - HALF + STRIP)
            match = match_ref[base : base + STRIP, tap : tap + 1]
            total = total + match * dpadded[rows] * s_ref[TAP + K - 1 - tap : TAP + K - tap]
            ds_ref[8 + tap : 9 + tap] += column_sum(center * (match * padded[rows]))
        dgated[base : base + STRIP] = total * match_ref[base : base + STRIP, K : K + 1]
    gate = jax.nn.sigmoid(u_ref[:, D:])
    dfirst = dgated[...] * gate
    dsecond = dfirst * u_ref[:, :D] * (1.0 - gate)
    ds_ref[6:7] = column_sum(dfirst)
    ds_ref[7:8] = column_sum(dsecond)
    xhat, inverse = normalize(a2_ref[...])
    normed = split(xhat * s_ref[4:5] + s_ref[5:6])
    dfirst = split(dfirst)
    dsecond = split(dsecond)
    dproj_ref[:, :D] = dot3(normed, dfirst, TN)
    dproj_ref[:, D:] = dot3(normed, dsecond, TN)
    dnormed = dot3(dfirst, split(proj_ref[:, :D]), NT) + dot3(dsecond, split(proj_ref[:, D:]), NT)
    ds_ref[0:1] = column_sum(dnormed * xhat)
    ds_ref[1:2] = column_sum(dnormed)
    da2_ref[...] = da3_ref[...] + normalize_back(dnormed * s_ref[4:5], xhat, inverse)


def convolution_backward(da3, a2, u, mixed, proj, weight, s, match):
    frames = a2.shape[0]
    vmem = pl.BlockSpec(memory_space=pltpu.VMEM)
    return pl.pallas_call(
        convolution_backward_kernel,
        in_specs=[vmem] * 8,
        out_specs=[vmem] * 4,
        out_shape=[
            jax.ShapeDtypeStruct((frames, D), f32),
            jax.ShapeDtypeStruct((D, 2 * D), f32),
            jax.ShapeDtypeStruct((D, D), f32),
            jax.ShapeDtypeStruct((24, D), f32),
        ],
        scratch_shapes=[
            pltpu.VMEM((frames + 2 * EDGE, D), f32),
            pltpu.VMEM((frames + 2 * EDGE, D), f32),
            pltpu.VMEM((frames, D), f32),
        ],
        compiler_params=pltpu.CompilerParams(vmem_limit_bytes=VMEM_LIMIT),
        name="convolution_backward",
    )(da3, a2, u, mixed, proj, weight, s, match)


def frame_tables(segments, valid_mask):
    packs, length = segments.shape
    position = jnp.arange(length, dtype=jnp.int32)
    columns = []
    for tap in range(K):
        moved = jnp.roll(segments, HALF - tap, axis=1)
        inside = (position + tap - HALF >= 0) & (position + tap - HALF < length)
        columns.append(((moved == segments) & inside[None, :]).astype(f32))
    columns.append(valid_mask.astype(f32))
    match = jnp.stack(columns, axis=-1).reshape(packs * length, K + 1)
    match = jnp.pad(match, ((0, 0), (0, 128 - K - 1)))
    segcol = jnp.broadcast_to(segments.reshape(packs * length, 1), (packs * length, 128))
    keyrow = jnp.pad(jnp.where(valid_mask > 0, segments, -1), ((0, -packs % 8), (0, 0)))
    return match, segcol, keyrow


def small_rows(parts):
    first, attend, conv, second = parts
    return jnp.concatenate(
        [
            first[0:2],
            attend[0:2],
            conv[0:2],
            conv[3:5],
            second[0:2],
            second[8:10],
            attend[5:7],
            attend[2:5],
            first[2:3],
            second[2:3],
            conv[6:8],
            conv[5:6],
            conv[2:3],
            first[4:8],
            second[4:8],
            conv[8 : 8 + K],
        ],
        axis=0,
    )


def layer(inputs, cotangent, segments, valid_mask, weights):
    feed_in, feed_out, square, proj, s = weights
    packs, length, _ = inputs.shape
    frames = packs * length
    x = inputs.reshape(frames, D)
    cot = cotangent.reshape(frames, D)
    match, segcol, keyrow = frame_tables(segments, valid_mask)
    pe = jnp.asarray(sinusoid_table(length))
    a1, u1 = ffn1_forward(x, feed_in[0], feed_out[0], s)
    a2, qkv, rel, probs, ctx = attention_forward(length, a1, square, pe, s, segcol, keyrow)
    a3, u, mixed = convolution_forward(a2, proj, square[5], s, match)
    out, da3, dwin2, dwout2, ds2 = ffn2(a3, cot, feed_in[1], feed_out[1], s)
    da2, dproj, dw5, dsc = convolution_backward(da3, a2, u, mixed, proj, square[5], s, match)
    da1, dw, dsa = attention_backward(length, da2, a1, qkv, rel, probs, ctx, square, pe, s)
    dx, dwin1, dwout1, ds1 = ffn1_backward(da1, x, u1, feed_in[0], feed_out[0], s)
    grads = (dwin1, dwin2), (dwout1, dwout2), (dw, dw5), dproj, small_rows((ds1, dsa, dsc, ds2))
    return out.reshape(inputs.shape), dx.reshape(inputs.shape), grads

MESH_ID = pl.DeviceIdType.MESH


def chip_grid(devices):
    side = 1
    while side * side * 2 * side * 2 < devices:
        side *= 2
    return side, side, 2 * side


class Place:
    def __init__(self, sizes):
        self.fsdp = sizes[1]
        self.y_size, self.x_size, self.z_size = chip_grid(sizes[0] * sizes[1])
        index = lax.axis_index("dp") * sizes[1] + lax.axis_index("fsdp")
        self.index = index
        self.core = lax.rem(index, 2)
        self.z = lax.rem(index // 2, self.z_size)
        self.x = lax.rem(index // (2 * self.z_size), 2)
        self.y = index // (4 * self.z_size)

    def device(self, y=None, x=None, z=None, core=None):
        y = self.y if y is None else y
        x = self.x if x is None else x
        z = self.z if z is None else z
        core = self.core if core is None else core
        index = ((y * 2 + x) * self.z_size + z) * 2 + core
        return index // self.fsdp, lax.rem(index, self.fsdp)

    def neighbour(self, axis):
        if axis == "core":
            return self.device(core=1 - self.core)
        if axis == "x":
            return self.device(x=1 - self.x)
        if axis == "y":
            return self.device(y=1 - self.y)
        return self.device(z=self.z + (1 if axis == "right" else -1))

    def greet(self):
        barrier = pltpu.get_barrier_semaphore()
        for axis in ("core", "x", "y"):
            pl.semaphore_signal(barrier, inc=1, device_id=self.neighbour(axis), device_id_type=MESH_ID)

        @pl.when(self.z > 0)
        def _():
            pl.semaphore_signal(barrier, inc=1, device_id=self.neighbour("left"), device_id_type=MESH_ID)

        @pl.when(self.z < self.z_size - 1)
        def _():
            pl.semaphore_signal(barrier, inc=1, device_id=self.neighbour("right"), device_id_type=MESH_ID)

        peers = 3 + (self.z > 0).astype(jnp.int32) + (self.z < self.z_size - 1).astype(jnp.int32)
        pl.semaphore_wait(barrier, peers)


EVERY = slice(None)


class Piece:
    def __init__(self, lead, first_row, rows, zfirst, near):
        self.lead, self.rows, self.zfirst, self.near = lead, pl.ds(first_row, rows), zfirst, near
        self.far = "y" if near == "x" else "x"

    def own(self, shard):
        return shard.at[self.rows] if self.lead is None else shard.at[self.lead, self.rows]

    def blocks(self, full, place, near, far, z, core):
        y, x = (near, far) if self.near == "y" else (far, near)
        index = (y, x, z, core, self.rows)
        return full.at[index] if self.lead is None else full.at[(self.lead,) + index]

    def here(self, place):
        return (place.x, place.y) if self.near == "x" else (place.y, place.x)


G_RIGHT, G_LEFT, G_NEAR, G_FAR, G_CORE = range(5)


class Gather:
    def __init__(self, place, piece, shard, full, send, recv, local):
        self.place, self.piece, self.shard, self.full = place, piece, shard, full
        self.send, self.recv, self.local = send, recv, local

    def view(self, near, far, z, core=None):
        return self.piece.blocks(self.full, self.place, near, far, z, self.place.core if core is None else core)

    def copy(self, kind, z, ref, axis, source=None):
        return pltpu.make_async_remote_copy(
            src_ref=ref if source is None else source,
            dst_ref=ref,
            send_sem=self.send.at[kind, z],
            recv_sem=self.recv.at[G_RIGHT if kind == G_LEFT else kind, z],
            device_id=self.place.neighbour(axis),
            device_id_type=MESH_ID,
        )

    def z_view(self, z):
        near, far = self.piece.here(self.place)
        return self.view(near if self.piece.zfirst else EVERY, far, z)

    def near_view(self, near, z):
        return self.view(near, self.piece.here(self.place)[1], z)

    def far_view(self, far, z):
        return self.view(EVERY, far, z)

    def core_view(self, core, z):
        return self.view(EVERY, EVERY, z, core)

    def own_copy(self):
        near, far = self.piece.here(self.place)
        return pltpu.make_async_copy(self.piece.own(self.shard), self.view(near, far, self.place.z), self.local)

    def begin(self):
        near, _ = self.piece.here(self.place)
        self.own_copy().start()
        own = self.piece.own(self.shard)
        if not self.piece.zfirst:
            self.copy(G_NEAR, self.place.z, self.near_view(near, self.place.z), self.piece.near, own).start()

    def z_send(self, z, source=None, right=True, left=True):
        place = self.place
        if right:

            @pl.when(place.z < place.z_size - 1)
            def _():
                self.copy(G_RIGHT, z, self.z_view(z), "right", source).start()

        if left:

            @pl.when(place.z > 0)
            def _():
                self.copy(G_LEFT, z, self.z_view(z), "left", source).start()

    def onward(self, z, source=None):
        near, far = self.piece.here(self.place)
        if self.piece.zfirst:
            self.copy(G_NEAR, z, self.near_view(near, z), self.piece.near, source).start()
        else:
            self.copy(G_FAR, z, self.far_view(far, z), self.piece.far).start()

    def at_distance(self, distance, step):
        place = self.place
        if distance == 0:
            step(place.z, None)
            return

        @pl.when(place.z >= distance)
        def _():
            step(place.z - distance, True)

        @pl.when(place.z + distance < place.z_size)
        def _():
            step(place.z + distance, False)

    def z_step(self, distance):
        near, _ = self.piece.here(self.place)

        def step(z, from_left):
            if from_left is None:
                if self.piece.zfirst:
                    own = self.piece.own(self.shard)
                    self.z_send(z, own)
                    self.onward(z, own)
                else:
                    self.copy(G_NEAR, z, self.near_view(1 - near, z), self.piece.near).wait_recv()
                    self.own_copy().wait()
                    self.z_send(z)
                    self.onward(z)
                return
            self.copy(G_RIGHT, z, self.z_view(z), "left").wait_recv()
            self.z_send(z, None, from_left, not from_left)
            self.onward(z)

        self.at_distance(distance, step)

    def near_step(self, distance):
        near, far = self.piece.here(self.place)

        def step(z, from_left):
            if from_left is None:
                self.own_copy().wait()
            self.copy(G_NEAR, z, self.near_view(1 - near, z), self.piece.near).wait_recv()
            self.copy(G_FAR, z, self.far_view(far, z), self.piece.far).start()

        if self.piece.zfirst:
            self.at_distance(distance, step)

    def far_step(self, distance):
        _, far = self.piece.here(self.place)

        def step(z, from_left):
            self.copy(G_FAR, z, self.far_view(1 - far, z), self.piece.far).wait_recv()
            self.copy(G_CORE, z, self.core_view(self.place.core, z), "core").start()

        self.at_distance(distance, step)

    def finish(self):
        place = self.place
        near, far = self.piece.here(place)
        for z in range(place.z_size):
            self.copy(G_CORE, z, self.core_view(1 - place.core, z), "core").wait_recv()
            self.copy(G_CORE, z, self.core_view(place.core, z), "core").wait_send()
            self.copy(G_FAR, z, self.far_view(far, z), self.piece.far).wait_send()
            if self.piece.zfirst:
                self.copy(G_NEAR, z, self.near_view(near, z), self.piece.near).wait_send()

            @pl.when((place.z < place.z_size - 1) & (z <= place.z))
            def _():
                self.copy(G_RIGHT, z, self.z_view(z), "right").wait_send()

            @pl.when((place.z > 0) & (z >= place.z))
            def _():
                self.copy(G_LEFT, z, self.z_view(z), "left").wait_send()

        if not self.piece.zfirst:
            self.copy(G_NEAR, place.z, self.near_view(near, place.z), self.piece.near).wait_send()


def gather_ticks(gathers, z_size):
    ticks = [[] for _ in range(z_size + 4)]
    for gather in gathers:
        ticks[0].append(gather.begin)
        shift = 0 if gather.piece.zfirst else 1
        for distance in range(z_size):
            ticks[distance + shift].append(functools.partial(gather.z_step, distance))
            ticks[distance + 1].append(functools.partial(gather.near_step, distance))
            ticks[distance + 2].append(functools.partial(gather.far_step, distance))
    ticks[-1] += [gather.finish for gather in gathers]
    return ticks


def halves(rows, zfirst, lead=None):
    return [Piece(lead, 0, rows // 2, zfirst, "x"), Piece(lead, rows // 2, rows // 2, zfirst, "y")]


def whole_shape(shard, sizes):
    y, x, z = chip_grid(sizes[0] * sizes[1])
    return shard.shape[:-2] + (y, x, z, 2) + shard.shape[-2:]


def gather_kernel(sizes, plans, offsets, *refs):
    arrays = sum(len(plan) for plan in plans)
    pieces = sum(len(p) for plan in plans for p in plan)
    shards, fulls = refs[:arrays], refs[arrays : 2 * arrays]
    send, recv, local = refs[2 * arrays :]
    place = Place(sizes)
    place.greet()
    schedule = {}
    array = count = 0
    for plan, offset in zip(plans, offsets):
        gathers = []
        for group in plan:
            for piece in group:
                gathers.append(Gather(place, piece, shards[array], fulls[array], send.at[count], recv.at[count], local.at[count]))
                count += 1
            array += 1
        for tick, steps in enumerate(gather_ticks(gathers, place.z_size)):
            schedule.setdefault(tick + offset, []).extend(steps)
    for tick in sorted(schedule):
        for step in schedule[tick]:
            step()


def gather(shards, plans, offsets, sizes, number, name):
    pieces = sum(len(p) for plan in plans for p in plan)
    z_size = chip_grid(sizes[0] * sizes[1])[2]
    return pl.pallas_call(
        functools.partial(gather_kernel, sizes, plans, offsets),
        in_specs=[pl.BlockSpec(memory_space=pltpu.VMEM)] * len(shards),
        out_specs=[pl.BlockSpec(memory_space=pl.ANY)] * len(shards),
        out_shape=[jax.ShapeDtypeStruct(whole_shape(shard, sizes), f32) for shard in shards],
        scratch_shapes=[
            pltpu.SemaphoreType.DMA((pieces, 5, z_size)),
            pltpu.SemaphoreType.DMA((pieces, 5, z_size)),
            pltpu.SemaphoreType.DMA((pieces,)),
        ],
        compiler_params=pltpu.CompilerParams(collective_id=number, has_side_effects=True, vmem_limit_bytes=VMEM_LIMIT),
        name=name,
    )(*shards)
S_CORE, S_FAR, S_NEAR, S_FROM_LEFT, S_FROM_RIGHT = range(5)


class Scatter:
    def __init__(self, place, piece, full, out, total, cores, fars, nears, lines, send, recv, local):
        self.place, self.piece, self.full, self.out = place, piece, full, out
        self.total, self.cores, self.fars, self.nears, self.lines = total, cores, fars, nears, lines
        self.send, self.recv, self.local = send, recv, local
        self.near, self.far = piece.here(place)

    def part(self, ref, near, far, z):
        y, x = (near, far) if self.piece.near == "y" else (far, near)
        index = (y, x, z)
        return ref.at[index] if self.piece.lead is None else ref.at[(EVERY,) + index]

    def staged(self, ref, *index):
        return ref.at[index] if self.piece.lead is None else ref.at[(EVERY,) + index]

    def add(self, target, source):
        target[...] = target[...] + source[...]

    def copy(self, kind, z, source, target, axis):
        return pltpu.make_async_remote_copy(
            src_ref=source,
            dst_ref=target,
            send_sem=self.send.at[kind, z],
            recv_sem=self.recv.at[kind, z],
            device_id=self.place.neighbour(axis),
            device_id_type=MESH_ID,
        )

    def core_copy(self, z):
        given = self.piece.blocks(self.full, self.place, EVERY, EVERY, z, 1 - self.place.core)
        return self.copy(S_CORE, z, given, self.part(self.cores, EVERY, EVERY, z), "core")

    def own_copy(self, z):
        kept = self.piece.blocks(self.full, self.place, EVERY, EVERY, z, self.place.core)
        return pltpu.make_async_copy(kept, self.part(self.total, EVERY, EVERY, z), self.local.at[z])

    def far_copy(self, z):
        return self.copy(S_FAR, z, self.part(self.total, EVERY, 1 - self.far, z), self.staged(self.fars, EVERY, z), self.piece.far)

    def near_copy(self, z):
        target = self.staged(self.nears, z if self.piece.zfirst else 0)
        return self.copy(S_NEAR, z, self.part(self.total, 1 - self.near, self.far, z), target, self.piece.near)

    def line_view(self, z):
        return self.part(self.total, self.near if self.piece.zfirst else EVERY, self.far, z)

    def line_staged(self, side, z):
        if self.piece.zfirst:
            return self.staged(self.lines, side, z)
        return self.staged(self.lines, side, EVERY, z)

    def line_copy(self, z, to_right):
        kind, side = (S_FROM_LEFT, 0) if to_right else (S_FROM_RIGHT, 1)
        return self.copy(kind, z, self.line_view(z), self.line_staged(side, z), "right" if to_right else "left")

    def begin(self):
        for distance in reversed(range(self.place.z_size)):
            for sign in (-1, 1) if distance else (1,):
                z = self.place.z + sign * distance

                @pl.when((z >= 0) & (z < self.place.z_size))
                def _():
                    self.core_copy(z).start()
                    self.own_copy(z).start()

    def core_step(self, z):
        self.core_copy(z).wait_recv()
        self.own_copy(z).wait()
        self.add(self.part(self.total, EVERY, EVERY, z), self.part(self.cores, EVERY, EVERY, z))

    def core_send(self, z):
        self.far_copy(z).start()

    def far_step(self, z):
        self.far_copy(z).wait_recv()
        self.add(self.part(self.total, EVERY, self.far, z), self.staged(self.fars, EVERY, z))

    def far_send(self, z):
        self.near_copy(z).start()

    def near_step(self, z):
        self.near_copy(z).wait_recv()
        self.add(self.part(self.total, self.near, self.far, z), self.staged(self.nears, z))

    def line_step(self, z):
        here = self.place.z

        @pl.when((z >= here) & (here > 0))
        def _():
            self.line_copy(z, True).wait_recv()
            self.add(self.line_view(z), self.line_staged(0, z))

        @pl.when((z <= here) & (here < self.place.z_size - 1))
        def _():
            self.line_copy(z, False).wait_recv()
            self.add(self.line_view(z), self.line_staged(1, z))

    def line_send(self, z):
        here = self.place.z

        @pl.when(z > here)
        def _():
            self.line_copy(z, True).start()

        @pl.when(z < here)
        def _():
            self.line_copy(z, False).start()

    def last_send(self):
        if not self.piece.zfirst:
            self.near_copy(self.place.z).start()

    def finish(self):
        z = self.place.z
        value = self.part(self.total, self.near, self.far, z)[...]
        if not self.piece.zfirst:
            self.near_copy(z).wait_recv()
            value = value + self.staged(self.nears, 0)[...]
        self.piece.own(self.out)[...] = value

    def drain(self):
        place = self.place
        for z in range(place.z_size):
            self.core_copy(z).wait_send()
            self.far_copy(z).wait_send()
            if self.piece.zfirst:
                self.near_copy(z).wait_send()

            @pl.when(z > place.z)
            def _():
                self.line_copy(z, True).wait_send()

            @pl.when(z < place.z)
            def _():
                self.line_copy(z, False).wait_send()

        if not self.piece.zfirst:
            self.near_copy(place.z).wait_send()


def scatter_stages(scatter):
    stages = [(scatter.core_step, scatter.core_send)]
    if scatter.piece.zfirst:
        return stages + [(scatter.far_step, scatter.far_send), (scatter.near_step, None), (scatter.line_step, scatter.line_send)]
    return stages + [(scatter.far_step, None), (scatter.line_step, scatter.line_send)]


def run_scatters(place, scatters, offsets, lag):
    blocks = 2 * place.z_size - 1
    for scatter in scatters:
        scatter.begin()
    staged = []
    for scatter, offset in zip(scatters, offsets):
        behind = offset
        for index, (work, send) in enumerate(scatter_stages(scatter)):
            staged.append((behind, work, send))
            behind += 0 if send is None else lag
    staged.sort(key=lambda stage: -stage[0])
    steps = max(stage[0] for stage in staged) + blocks

    def body(step, carry):
        for action in (1, 2):
            for stage in staged:
                if stage[action] is None:
                    continue
                item = step - stage[0]
                distance = place.z_size - 1 - item // 2
                z = place.z + jnp.where(lax.rem(item, 2) == 0, -distance, distance)

                @pl.when((item >= 0) & (item < blocks) & (z >= 0) & (z < place.z_size))
                def _():
                    stage[action](z)

        return carry

    lax.fori_loop(0, steps, body, 0)
    for scatter in scatters:
        scatter.last_send()
    for scatter in scatters:
        scatter.finish()
    for scatter in scatters:
        scatter.drain()


def scatter_scratch(piece, columns, place_sizes, lead):
    y, x, z = chip_grid(place_sizes[0] * place_sizes[1])
    rows = piece.rows.size
    head = () if piece.lead is None else (lead,)
    return [
        pltpu.VMEM(head + (y, x, z, rows, columns), f32),
        pltpu.VMEM(head + (y, x, z, rows, columns), f32),
        pltpu.VMEM(head + (2, z, rows, columns), f32),
        pltpu.VMEM(head + ((z,) if piece.zfirst else (1,)) + (rows, columns), f32),
        pltpu.VMEM(head + ((2, z) if piece.zfirst else (2, 2, z)) + (rows, columns), f32),
    ]


def scatter_kernel(sizes, plans, starts, lag, total_norm, *refs):
    arrays = sum(len(plan) for plan in plans)
    pieces = sum(len(p) for plan in plans for p in plan)
    fulls, refs = refs[:arrays], refs[arrays:]
    outs, refs = refs[:arrays], refs[arrays:]
    if total_norm:
        norms, refs = refs[0], refs[1:]
    scratch, refs = refs[: 5 * pieces], refs[5 * pieces :]
    send, recv, local = refs[:3]
    place = Place(sizes)
    if total_norm:
        greet_all(place, sizes)
    else:
        place.greet()
    scatters, offsets = [], []
    array = count = 0
    for plan, start in zip(plans, starts):
        for group in plan:
            for piece in group:
                scatters.append(
                    Scatter(place, piece, fulls[array], outs[array], *scratch[5 * count : 5 * count + 5], send.at[count], recv.at[count], local.at[count])
                )
                offsets.append(start)
                count += 1
            array += 1
    run_scatters(place, scatters, offsets, lag)
    if total_norm:
        share_norm(place, sizes, outs, norms, *refs[3:])


def greet_all(place, sizes):
    devices = sizes[0] * sizes[1]
    barrier = pltpu.get_barrier_semaphore()

    def signal(offset, carry):
        other = lax.rem(place.index + offset, devices)
        pl.semaphore_signal(barrier, inc=1, device_id=(other // sizes[1], lax.rem(other, sizes[1])), device_id_type=MESH_ID)
        return carry

    lax.fori_loop(1, devices, signal, 0)
    pl.semaphore_wait(barrier, devices - 1)


def square_tile(values):
    squares = values * values
    tile = jnp.zeros((8, 128), f32)
    for r in range(0, values.shape[0], 8):
        for c in range(0, values.shape[1], 128):
            tile = tile + squares[r : r + 8, c : c + 128]
    return tile


def share_norm(place, sizes, outs, norms, own, send, recv):
    devices = sizes[0] * sizes[1]
    tile = jnp.zeros((8, 128), f32)
    for out in outs:
        for lead in range(out.shape[0]) if len(out.shape) == 3 else (None,):
            tile = tile + square_tile(out[...] if lead is None else out[lead])
    own[...] = tile
    norms[place.index] = tile

    def copy(offset, to):
        other = lax.rem(place.index + offset, devices)
        slot = place.index if to else other
        return pltpu.make_async_remote_copy(
            src_ref=own,
            dst_ref=norms.at[slot],
            send_sem=send.at[other],
            recv_sem=recv.at[slot],
            device_id=(other // sizes[1], lax.rem(other, sizes[1])),
            device_id_type=MESH_ID,
        )

    lax.fori_loop(1, devices, lambda offset, carry: (copy(offset, True).start(), carry)[1], 0)
    lax.fori_loop(1, devices, lambda offset, carry: (copy(offset, False).wait_recv(), carry)[1], 0)
    lax.fori_loop(1, devices, lambda offset, carry: (copy(offset, True).wait_send(), carry)[1], 0)


def shard_shape(full):
    return full.shape[:-6] + full.shape[-2:]


def scatter(fulls, plans, starts, lag, sizes, number, name, total_norm):
    devices = sizes[0] * sizes[1]
    pieces = sum(len(p) for plan in plans for p in plan)
    z_size = chip_grid(devices)[2]
    scratch = []
    array = 0
    for plan in plans:
        for group in plan:
            for piece in group:
                lead = None if piece.lead is None else piece.lead.size
                scratch += scatter_scratch(piece, fulls[array].shape[-1], sizes, lead)
            array += 1
    vmem = pl.BlockSpec(memory_space=pltpu.VMEM)
    shapes = [jax.ShapeDtypeStruct(shard_shape(full), f32) for full in fulls]
    sems = [
        pltpu.SemaphoreType.DMA((pieces, 5, z_size)),
        pltpu.SemaphoreType.DMA((pieces, 5, z_size)),
        pltpu.SemaphoreType.DMA((pieces, z_size)),
    ]
    if total_norm:
        shapes.append(jax.ShapeDtypeStruct((devices, 8, 128), f32))
        sems += [pltpu.VMEM((8, 128), f32), pltpu.SemaphoreType.DMA((devices,)), pltpu.SemaphoreType.DMA((devices,))]
    return pl.pallas_call(
        functools.partial(scatter_kernel, sizes, plans, starts, lag, total_norm),
        in_specs=[pl.BlockSpec(memory_space=pl.ANY)] * len(fulls),
        out_specs=[vmem] * len(shapes),
        out_shape=shapes,
        scratch_shapes=scratch + sems,
        compiler_params=pltpu.CompilerParams(collective_id=number, has_side_effects=True, vmem_limit_bytes=VMEM_LIMIT),
        name=name,
    )(*fulls)


def adamw_kernel(step_ref, norms_ref, *refs):
    (g_in1, g_in2, g_out1, g_out2, g_sq, g_conv, g_small), refs = refs[:7], refs[7:]
    weights, firsts, seconds, outs = refs[0:5], refs[5:10], refs[10:15], refs[16:]
    norm = jnp.sqrt(jnp.sum(norms_ref[...], axis=(0, 1, 2), keepdims=True)[0])
    refs[15][...] = norm
    clip = jnp.minimum(1.0, CLIP_NORM / (norm + 1e-06))

    def geometric(_, carry):
        one, one_power, two, two_power = carry
        return one + one_power, one_power * BETA_ONE, two + two_power, two_power * BETA_TWO

    zero, unit = jnp.float32(0.0), jnp.float32(1.0)
    one, _, two, _ = lax.fori_loop(0, step_ref[0], geometric, (zero, unit, zero, unit))
    first_scale = jnp.full((1, 1), (1.0 - BETA_ONE) * one, f32)
    second_scale = jnp.full((1, 1), (1.0 - BETA_TWO) * two, f32)
    first_scale = 1.0 / first_scale
    second_scale = 1.0 / second_scale

    def update(number, index, gradient, rate, decay):
        weight, first, second = weights[number][index], firsts[number][index], seconds[number][index]
        clipped = clip * gradient
        first_next = BETA_ONE * first + (1.0 - BETA_ONE) * clipped
        second_next = BETA_TWO * second + (1.0 - BETA_TWO) * clipped * clipped
        step = (first_next * first_scale) / (jnp.sqrt(second_next * second_scale) + ADAM_EPS)
        if decay:
            step = step + decay * weight
        outs[3 * number][index] = first_next
        outs[3 * number + 1][index] = second_next
        outs[3 * number + 2][index] = weight - rate * step

    for half, (g_in, g_out) in enumerate(((g_in1, g_out1), (g_in2, g_out2))):
        update(0, half, g_in[...], MATRIX_RATE, MATRIX_DECAY)
        update(1, half, g_out[...], MATRIX_RATE, MATRIX_DECAY)
    for index in range(6):
        update(2, index, g_sq[index], MATRIX_RATE, MATRIX_DECAY)
    update(3, EVERY, g_conv[...], MATRIX_RATE, MATRIX_DECAY)
    update(4, EVERY, g_small[...], VECTOR_RATE, 0.0)


def adamw(step, norms, grads, weights, firsts, seconds):
    vmem = pl.BlockSpec(memory_space=pltpu.VMEM)
    shapes = [jax.ShapeDtypeStruct((1, 1), f32)]
    for weight in weights:
        shapes += [jax.ShapeDtypeStruct(weight.shape, f32)] * 3
    return pl.pallas_call(
        adamw_kernel,
        in_specs=[pl.BlockSpec(memory_space=pltpu.SMEM)] + [vmem] * 23,
        out_specs=[vmem] * 16,
        out_shape=shapes,
        compiler_params=pltpu.CompilerParams(vmem_limit_bytes=VMEM_LIMIT),
        name="adamw",
    )(step, norms, *grads, *weights, *firsts, *seconds)


AXES = ("dp", "fsdp")
SMALL_LANES = 128


def plans():
    feed = [halves(16, False), halves(64, True)]
    small = [Piece(None, 0, 16, False, "x")]
    square = [
        Piece(pl.ds(0, 4), 0, 8, False, "x"),
        Piece(pl.ds(0, 4), 8, 8, False, "y"),
        Piece(pl.ds(4, 2), 0, 8, True, "x"),
        Piece(pl.ds(4, 2), 8, 8, True, "y"),
    ]
    return [small] + feed, [square, halves(16, True)], feed


def gather_weights(sizes, feed_in, feed_out, square, proj, small):
    first, middle, last = plans()
    small = jnp.pad(small.T, ((0, 0), (0, SMALL_LANES - small.shape[0])))
    shards = [small, feed_in[0], feed_out[0], square, proj, feed_in[1], feed_out[1]]
    s, in1, out1, sq, conv, in2, out2 = gather(shards, [first, middle, last], (0, 1, 2), sizes, 0, "gather_weights")
    return (
        (in1.reshape(D, FF), in2.reshape(D, FF)),
        (out1.reshape(FF, D), out2.reshape(FF, D)),
        sq.reshape(6, D, D),
        conv.reshape(D, 2 * D),
        s.reshape(D, SMALL_LANES).T,
    )


def scatter_gradients(sizes, grads):
    (in1, in2), (out1, out2), (dw, dw5), dproj, ds = grads
    grid = chip_grid(sizes[0] * sizes[1]) + (2,)
    first, middle, last = plans()
    ds = jnp.pad(ds, ((0, SMALL_LANES - ds.shape[0]), (0, 0))).T

    def split_rows(full):
        rows = full.shape[-2] // (sizes[0] * sizes[1])
        return full.reshape(full.shape[:-2] + grid + (rows, full.shape[-1]))

    fulls = [split_rows(v) for v in (in2, out2, jnp.concatenate([dw, dw5[None]]), dproj, ds, in1, out1)]
    g_in2, g_out2, g_sq, g_conv, g_s, g_in1, g_out1, norms = scatter(
        fulls, [last, middle, first], (0, 4, 8), 2, sizes, 1, "scatter_gradients", True
    )
    return (g_in1, g_in2, g_out1, g_out2, g_sq, g_conv, g_s), norms


def gather_plain(feed_in, feed_out, square, proj, small):
    feed_in = lax.all_gather(feed_in, AXES, axis=1, tiled=True)
    feed_out = lax.all_gather(feed_out, AXES, axis=1, tiled=True)
    square = lax.all_gather(square, AXES, axis=1, tiled=True)
    proj = lax.all_gather(proj, AXES, axis=0, tiled=True)
    small = lax.all_gather(small, AXES, axis=1, tiled=True)
    return feed_in, feed_out, square, proj, small


def scatter_plain(grads):
    (in1, in2), (out1, out2), (dw, dw5), dproj, ds = grads
    parts = [lax.psum_scatter(v, AXES, scatter_dimension=0, tiled=True) for v in (in1, in2, out1, out2)]
    parts.append(lax.psum_scatter(jnp.concatenate([dw, dw5[None]]), AXES, scatter_dimension=1, tiled=True))
    parts.append(lax.psum_scatter(dproj, AXES, scatter_dimension=0, tiled=True))
    parts.append(lax.psum_scatter(ds, AXES, scatter_dimension=1, tiled=True))
    total = lax.psum(sum(jnp.sum(part * part) for part in parts), AXES)
    return tuple(parts), jnp.zeros((1, 8, 128), f32).at[0, 0, 0].set(total)


def local(sizes, inputs, cotangent, segments, valid_mask, step_count, *state):
    weights, moments = state[:5], state[5:]
    firsts, seconds = moments[0::2], moments[1::2]
    devices = sizes[0] * sizes[1]
    kernels = D // devices % 16 == 0 and chip_grid(devices)[:2] == (2, 2)
    full = gather_weights(sizes, *weights) if kernels else gather_plain(*weights)
    out, dx, grads = layer(inputs, cotangent, segments, valid_mask, full)
    if kernels:
        grads, norms = scatter_gradients(sizes, grads)
        grads = grads[:6] + (grads[6].T[: weights[4].shape[0]],)
    else:
        grads, norms = scatter_plain(grads)
    norm, *updated = adamw(step_count, norms, grads, weights, firsts, seconds)
    return (out, dx, norm.reshape(()), *updated)


def solution(mesh):
    sizes = (mesh.shape["dp"], mesh.shape["fsdp"])
    batch = P(AXES, None, None)
    rows = P(AXES, None)
    middle = P(None, AXES, None)
    columns = P(None, AXES)
    weights = (middle, middle, middle, rows, columns)
    moments = tuple(spec for spec in weights for _ in range(2))
    return jax.shard_map(
        functools.partial(local, sizes),
        mesh=mesh,
        in_specs=(batch, batch, rows, rows, P()) + weights + moments,
        out_specs=(batch, batch, P()) + tuple(spec for spec in weights for _ in range(3)),
        check_vma=False,
    )
```

time: 1800 us -> 433 us (0.24)
  waiting for transfers between devices: 913 us -> 0 us
  matrix products: 409 us -> 0 us
  Pallas kernels: 0 us -> 387 us
  local copies, waits for them, and re-layouts: 266 us -> 28.9 us
  blocking collectives: 82 us -> 0 us
  other arithmetic: 86.4 us -> 8.73 us
  between operations: 20 us -> 1.78 us
    reduce_scatter x5 -> x0, waiting for transfers between devices: 669 us -> none  [the longest x1 152 us: local(): lax.psum_scatter(grad_in, ('dp', 'fsdp'), scatter_dimension=1, tiled=True)]
    dot_general x113 -> x0, matrix products: 409 us -> none  [the longest x85 312 us: matmul(): jnp.dot(left, right, precision=PRECISE, preferred_element_type=jnp.float32)]
    pallas_call x0 -> x10, Pallas kernels: none -> 387 us  [the longest x1 132 us: scatter(): pl.pallas_call(functools.partial(scatter_kernel, sizes, plans, starts, la...]
    all_gather x4 -> x0, waiting for transfers between devices: 239 us -> none  [the longest x1 79.4 us: local(): lax.all_gather(feed_in, ('dp', 'fsdp'), axis=1, tiled=True)]
    while x533 -> x0, local copies, waits for them, and re-layouts: 96.2 us -> none
    reshape x20 -> x1, local copies, waits for them, and re-layouts: 61.6 us -> 1.79 us  [gather_weights(): s.reshape(D, SMALL_LANES)]
    all_gather x1 -> x0, blocking collectives: 45.1 us -> none  [local(): lax.all_gather(small_params, ('dp', 'fsdp'), axis=1, tiled=True)]
    psum x1 -> x0, blocking collectives: 36.9 us -> none  [local(): gradient_norm = jnp.sqrt(lax.psum(partial_sum, ('dp', 'fsdp')))]
  transfers between devices with their start and end apart: 9 -> 0, of which waited for: 9 -> 0; matrix products, arithmetic and copies ran while one was open for 1% -> 0% of each run, Pallas kernels for 0% -> 0%
where the time goes in v1:
time: 433 us; the launch traced here: 426 us
  Pallas kernels  387 us (89%)
  local copies, waits for them, and re-layouts  28.9 us (7%)
  other arithmetic  8.73 us (2%)
    pallas_call x1, Pallas kernels, scatter(): pl.pallas_call(functools.partial(scatter_kernel, sizes, plans, starts, la...  132 us
    pallas_call x1, Pallas kernels, gather(): pl.pallas_call(functools.partial(gather_kernel, sizes, plans, offsets), i...  105 us
    pallas_call x1, Pallas kernels, attention_backward(): pl.pallas_call(functools.partial(attention_backward_kernel, length), in_s...  38.5 us
    pallas_call x1, Pallas kernels, ffn2(): pl.pallas_call(ffn2_kernel, grid=(2 * NC,), in_specs=[whole, whole, pl.Bl...  30.6 us
    pallas_call x1, Pallas kernels, attention_forward(): pl.pallas_call(functools.partial(attention_forward_kernel, length), in_sp...  21.7 us
    pallas_call x1, Pallas kernels, ffn1_backward(): pl.pallas_call(ffn1_backward_kernel, grid=(NC,), in_specs=[whole, whole,...  21.7 us
    pallas_call x1, Pallas kernels, convolution_backward(): pl.pallas_call(convolution_backward_kernel, in_specs=[vmem] * 8, out_spec...  14.5 us
    pallas_call x1, Pallas kernels, ffn1_forward(): pl.pallas_call(ffn1_forward_kernel, grid=(NC,), in_specs=[whole, pl.Block...  11.2 us

profile of v1, /device:TPU:0, one launch (start us, length us, event | category | flops | bytes accessed | tf_op | source)
XLA Modules:
  0.0 426.5 jit_solution(13963978965284565016)
XLA Ops:
  0.7 0.8 fusion.12
  1.5 0.8 fusion.14
  2.3 0.8 fusion.16
  3.1 0.8 fusion.18
  4.0 0.8 fusion.13
  4.7 0.8 fusion.15
  5.5 0.8 fusion.17
  6.3 0.8 fusion.19
  7.1 0.8 fusion.7
  8.7 0.8 convert_bitcast_fusion
  10.4 1.7 slice_bitcast_fusion
  12.1 1.7 slice_bitcast_fusion.1
  13.8 1.3 pad.16.refs_0_
  15.1 104.6 %gather_weights.1 = (f32[2,2,4,2,16,128]{5,4,3,2,1,0:T(8,128)}, f32[2,2,4,2,16,2048]{5,4,3,2,1,0:T(8,128)}, f32[2,2,4,2,64,512]{5,4,3,2,1,0:T(8,128)}, f32[6,2,2...) custom-call(f32[16,128]{1,0:T(8,128)} %pad.16.refs_0_, ...), custom_call_target="tpu_custom_call" | custom-call | tf_op jit(solution)/shard_map/gather_weights/pallas_call | solution.py:881
  119.7 1.8 copy.67
  121.5 11.2 %ffn1_forward.1 = (f32[512,512]{1,0:T(8,128)}, f32[512,2048]{1,0:T(8,128)}) custom-call(f32[512,512]{1,0:T(8,128)} %bitcast.104, f32[512,2048]{1,0:T(8,128)} %bitcast.95, f32[2048,512]{1,0:T(8,128)} %bitcast.97, f32[128,512]{1,0:T(8,128)} %bitcast.88), custom_call_target="tpu_custom_call" | custom-call | tf_op jit(solution)/shard_map/ffn1_forward/pallas_call | solution.py:110
  133.3 0.8 broadcast_in_dim.8.segcol_ref
  134.2 21.7 %attention_forward.1 = (f32[512,512]{1,0:T(8,128)}, f32[3,512,512]{2,1,0:T(8,128)}, f32[256,512]{1,0:T(8,128)}, f32[16,256,256]{2,1,0:T(8,128)}, f32[512,512]{1,0:T(8,128)}) custom-call(f32[512,512]{1,0:T(8,128)} %get-tuple-element.78.a1_ref, f32[6,512,512]{2,1,0:T(8,128)} %bitcast.86, f32[2,256,512]{2,1,0:T(8,128)} %constant.46.clone.pe_ref, ...), custom_call_target="tpu_custom_call" | custom-call | tf_op jit(solution)/shard_map/attention_forward/pallas_call | solution.py:323
  155.9 2.3 slice.136
  158.2 8.2 %convolution_forward.1 = (f32[512,512]{1,0:T(8,128)}, f32[512,1024]{1,0:T(8,128)}, f32[512,512]{1,0:T(8,128)}) custom-call(f32[512,512]{1,0:T(8,128)} %get-tuple-element.80.a2_ref, f32[512,1024]{1,0:T(8,128)} %bitcast.101, f32[512,512]{1,0:T(8,128)} %bitcast.99, f32[128,512]{1,0:T(8,128)} %bitcast.90, f32[512,128]{1,0:T(8,128)} %pad.18.match_ref), custom_call_target="tpu_custom_call" | custom-call | tf_op jit(solution)/shard_map/convolution_forward/pallas_call | solution.py:467
  166.5 30.6 %ffn2.1 = (f32[512,512]{1,0:T(8,128)}, f32[512,512]{1,0:T(8,128)}, f32[512,2048]{1,0:T(8,128)}, f32[2048,512]{1,0:T(8,128)}, f32[16,512]{1,0:T(8,128)}) custom-call(f32[512,512]{1,0:T(8,128)} %get-tuple-element.82.a3_ref, f32[512,512]{1,0:T(8,128)} %bitcast.115, f32[512,2048]{1,0:T(8,128)} %bitcast.110, f32[2048,512]{1,0:T(8,128)} %bitcast.111, ...), custom_call_target="tpu_custom_call" | custom-call | tf_op jit(solution)/shard_map/ffn2/pallas_call | solution.py:226
  197.0 14.5 %convolution_backward.1 = (f32[512,512]{1,0:T(8,128)}, f32[512,1024]{1,0:T(8,128)}, f32[512,512]{1,0:T(8,128)}, f32[24,512]{1,0:T(8,128)}) custom-call(f32[512,512]{1,0:T(8,128)} %get-tuple-element.86.da3_ref, f32[512,512]{1,0:T(8,128)} %get-tuple-element.80.a2_ref, f32[512,1024]{1,0:T(8,128)} %get-tuple-element.87.u_ref, ...), custom_call_target="tpu_custom_call" | custom-call | tf_op jit(solution)/shard_map/convolution_backward/pallas_call | solution.py:535
  211.5 38.5 %attention_backward.1 = (f32[512,512]{1,0:T(8,128)}, f32[5,512,512]{2,1,0:T(8,128)}, f32[8,512]{1,0:T(8,128)}) custom-call(f32[512,512]{1,0:T(8,128)} %get-tuple-element.89.da2_ref, f32[512,512]{1,0:T(8,128)} %get-tuple-element.78.a1_ref, f32[3,512,512]{2,1,0:T(8,128)} %get-tuple-element.90.qkv_ref, f32[256,512]{1,0:T(8,128)} %get-tuple-element.91.rel_ref, ...), custom_call_target="tpu_custom_call" | custom-call | tf_op jit(solution)/shard_map/attention_backward/pallas_call | solution.py:417
  250.0 21.7 %ffn1_backward.1 = (f32[512,512]{1,0:T(8,128)}, f32[512,2048]{1,0:T(8,128)}, f32[2048,512]{1,0:T(8,128)}, f32[8,512]{1,0:T(8,128)}) custom-call(f32[512,512]{1,0:T(8,128)} %get-tuple-element.94.da_ref, f32[512,512]{1,0:T(8,128)} %bitcast.105, f32[512,2048]{1,0:T(8,128)} %get-tuple-element.95.u_ref, f32[512,2048]{1,0:T(8,128)} %bitcast.96, ...), custom_call_target="tpu_custom_call" | custom-call | tf_op jit(solution)/shard_map/ffn1_backward/pallas_call | solution.py:160
  274.6 0.8 copy.69
  275.5 6.4 %pad_maximum_fusion.refs_2_ = f32[6,2,2,4,2,16,512]{6,5,4,3,2,1,0:T(8,128)} fusion(f32[1,2,2,4,2,16,512]{6,5,4,3,2,1,0:T(8,128)S(1)} %bitcast.114, f32[5,2,2,4,2,16,512]{6,5,4,3,2,1,0:T(8,128)} %bitcast.103), kind=kLoop, calls=%fused_computation | loop fusion | flops 1572864 | bytes 12582912 | tf_op jit(solution)/shard_map/concatenate | solution.py:1303
  281.9 132.1 %scatter_gradients.1 = (f32[16,2048]{1,0:T(8,128)}, f32[64,512]{1,0:T(8,128)}, f32[6,16,512]{2,1,0:T(8,128)}, f32[16,1024]{1,0:T(8,128)}, f32[16,128]{1,0:T(8,12...) custom-call(f32[2,2,4,2,16,2048]{5,4,3,2,1,0:T(8,128)} %bitcast.106, ...), custom_call_target="tpu_custom_call" | custom-call | tf_op jit(solution)/shard_map/scatter_gradients/pallas_call | solution.py:1198
  414.0 0.8 copy.70
  418.1 3.9 adamw.1
  422.0 1.4 copy.74
  423.4 1.4 copy.75
  424.8 1.4 copy.76
  (55 shorter events, 7.9 us)
Async XLA Ops:
  121.5 11.8 %copy-start.1 = (s32[2,256]{1,0:T(2,128)S(1)}, s32[2,256]{1,0:T(2,128)}, u32[]{:S(2)}) copy-start(s32[2,256]{1,0:T(2,128)} %param.23) | copy-start | bytes 6148
  250.0 23.9 %copy-start.4 = (f32[8,512]{1,0:T(8,128)S(1)}, f32[8,512]{1,0:T(8,128)}, u32[]{:S(2)}) copy-start(f32[8,512]{1,0:T(8,128)} %get-tuple-element.103) | copy-start | bytes 49156
  250.0 23.9 %copy-start.2 = (f32[24,512]{1,0:T(8,128)S(1)}, f32[24,512]{1,0:T(8,128)}, u32[]{:S(2)}) copy-start(f32[24,512]{1,0:T(8,128)} %get-tuple-element.104) | copy-start | bytes 147460
  250.0 24.0 %copy-start.5 = (f32[16,512]{1,0:T(8,128)S(1)}, f32[16,512]{1,0:T(8,128)}, u32[]{:S(2)}) copy-start(f32[16,512]{1,0:T(8,128)} %get-tuple-element.105) | copy-start | bytes 98308
  250.0 25.5 %copy-start = (f32[512,512]{1,0:T(8,128)S(1)}, f32[512,512]{1,0:T(8,128)}, u32[]{:S(2)}) copy-start(f32[512,512]{1,0:T(8,128)} %get-tuple-element.100) | copy-start | bytes 3145732
  281.9 133.5 %copy-start.3 = (f32[40,16]{0,1:T(8,128)S(1)}, f32[40,16]{0,1:T(8,128)}, u32[]{:S(2)}) copy-start(f32[40,16]{0,1:T(8,128)} %param.30) | copy-start | bytes 7684
  281.9 134.2 %copy-start.6 = (f32[40,16]{0,1:T(8,128)S(1)}, f32[40,16]{0,1:T(8,128)}, u32[]{:S(2)}) copy-start(f32[40,16]{0,1:T(8,128)} %param.39) | copy-start | bytes 7684
  281.9 134.9 %copy-start.7 = (f32[40,16]{0,1:T(8,128)S(1)}, f32[40,16]{0,1:T(8,128)}, u32[]{:S(2)}) copy-start(f32[40,16]{0,1:T(8,128)} %param.40) | copy-start | bytes 7684
